TPU v7x, 128 devices: a whole 4x4x4 slice. The times are simulated.
128 devices in a mesh: head: 8 (over x_hi, z), ctx: 16 (over y, x_lo, core).
Axes of the slice: x: 4 (x_hi: 2, x_lo: 2; x = x_hi * 2 + x_lo), y: 4, z: 4, core: 2. Of those that a mesh axis runs over, the one named last changes fastest.
Arguments:
- inputs: bfloat16 [4096, 4096], P('ctx'), may hold values from -8 to 8
- out_grad: bfloat16 [4096, 4096], P('ctx', 'head'), may hold values from -6 to 6
- w_query: bfloat16 [4096, 4096], P(None, 'head'), may hold values from -4 to 4
- w_key: bfloat16 [4096, 1024], P(None, 'head'), may hold values from -4 to 4
- value_projection: bfloat16 [4096, 1024], P(None, 'head'), may hold values from -0.09375 to 0.09375
- w_out: bfloat16 [4096, 4096], P('head'), may hold values from -0.09375 to 0.09375
- doc_lengths: int32 [8], replicated, may hold values from 1 to 2048, 4096 in all
- span_order: int32 [32], replicated, may hold values from 0 to 31, as said below
Outputs:
- input_grad: bfloat16 [4096, 4096], P('ctx', 'head')
Inputs may be any that keep to these rules, and one draw needn't show every extreme that they name: `span_order`: A permutation of 0 to 31; entries 2 d and 2 d + 1 are c and 31 - c for some c, in either order.
All inputs are finite; a program needn't handle non-finite values.
Results may differ from a plain program's by a relative error of at most 0.012.
The roundings to bfloat16 on the way count: a program that leaves them out, or rounds other values in their place, can miss the bound.
Values may be sent and summed in bfloat16 or wider, within the bound.
A program may use at most 64 MiB of HBM per device.

v0:
```python
import math

import jax
import jax.numpy as jnp
from jax import lax
from jax.experimental import pallas as pl
from jax.experimental.pallas import tpu as pltpu
from jax.sharding import PartitionSpec as P

ASKER_NUM = 32
SHARED_KV_NUM = 8
CHANNEL_DIM = 128
BUNDLE = ASKER_NUM // SHARED_KV_NUM
HALF = 128
TILE = 256
RING = 4
FEATURES = 512
CHUNKS = 4
OFFSETS = ((2, 1), (2, 0), (1, 1), (3, 1), (1, 0), (3, 0), (0, 1))
LOG2E = 1.4426950408889634
MASKED = -1e30
MESH = pl.DeviceIdType.MESH


def remote(src, dst, send, receive, place):
    return pltpu.make_async_remote_copy(
        src_ref=src, dst_ref=dst, send_sem=send, recv_sem=receive,
        device_id=place, device_id_type=MESH,
    )


def greet(places):
    barrier = pltpu.get_barrier_semaphore()
    for place in places:
        pl.semaphore_signal(barrier, inc=1, device_id=place, device_id_type=MESH)
    pl.semaphore_wait(barrier, len(places))


def neighbours():
    head = lax.axis_index("head")
    ctx = lax.axis_index("ctx")
    far, depth = head // RING, head % RING
    line, near, core = ctx // 4, (ctx // 2) % 2, ctx % 2

    def head_of(f, d):
        return f * RING + d

    def ctx_of(r, n, c):
        return r * 4 + n * 2 + c

    places = {
        "head_up": (head_of(far, (depth + 1) % RING), ctx),
        "head_down": (head_of(far, (depth + 3) % RING), ctx),
        "head_pair": (head_of(1 - far, depth), ctx),
        "ctx_up": (head, ctx_of((line + 1) % RING, near, core)),
        "ctx_down": (head, ctx_of((line + 3) % RING, near, core)),
        "ctx_pair": (head, ctx_of(line, 1 - near, core)),
        "sibling": (head, ctx_of(line, near, 1 - core)),
    }
    return places, (far, depth), (line, near, core)


class Gather:
    def __init__(self, source, block, half, pair, ring, sends, receives, up, down, across):
        other = 1 - pair
        before, after, opposite = (ring + 3) % RING, (ring + 1) % RING, (ring + 2) % RING
        self.copies = []
        own = block(pair, ring)
        plan = [
            (source(0), half(pair, ring, 0), half(pair, before, 0), up),
            (source(1), half(pair, ring, 1), half(pair, after, 1), down),
            (source(None), own, block(other, ring), across),
            (source(1), half(pair, ring, 1), half(pair, before, 1), up),
            (source(0), half(pair, ring, 0), half(pair, after, 0), down),
            (half(pair, before, 0), half(pair, before, 0), half(pair, opposite, 0), up),
            (half(pair, after, 1), half(pair, after, 1), half(pair, opposite, 1), down),
            (half(other, ring, 0), half(other, ring, 0), half(other, before, 0), up),
            (half(other, ring, 1), half(other, ring, 1), half(other, after, 1), down),
            (half(other, ring, 1), half(other, ring, 1), half(other, before, 1), up),
            (half(other, ring, 0), half(other, ring, 0), half(other, after, 0), down),
            (half(other, before, 0), half(other, before, 0), half(other, opposite, 0), up),
            (half(other, after, 1), half(other, after, 1), half(other, opposite, 1), down),
        ]
        for k, (src, dst, landed, place) in enumerate(plan):
            self.copies.append(
                (
                    remote(src, dst, sends.at[k], receives.at[k], place),
                    remote(landed, landed, sends.at[k], receives.at[k], place),
                )
            )

    def start(self, *which):
        for k in which:
            self.copies[k][0].start()

    def arrive(self, *which):
        for k in which:
            self.copies[k][1].wait_recv()

    def drain(self):
        for sent, landed in self.copies:
            sent.wait_send()


def front_kernel(
    x_hbm, og_hbm, wq_hbm, wk_hbm, wv_hbm, wo_hbm,
    q_ref, g_ref, kv_ref,
    x, wq, wkv, wo, og, acc,
    loads, head_send, head_receive, ctx_send, ctx_receive, sibling_send, sibling_receive,
):
    places, (far, depth), (line, near, core) = neighbours()
    me = far * RING + depth
    local = [
        pltpu.make_async_copy(x_hbm, x, loads.at[0]),
        pltpu.make_async_copy(wk_hbm, wkv.at[:, :CHANNEL_DIM], loads.at[1]),
        pltpu.make_async_copy(wv_hbm, wkv.at[:, CHANNEL_DIM:], loads.at[2]),
        pltpu.make_async_copy(wq_hbm, wq, loads.at[3]),
        pltpu.make_async_copy(og_hbm, og.at[me], loads.at[4]),
        pltpu.make_async_copy(wo_hbm, wo, loads.at[5]),
    ]
    for copy in local:
        copy.start()
    greet(list(places.values()))

    heads = Gather(
        lambda k: og_hbm if k is None else og_hbm.at[pl.ds(k * HALF, HALF), :],
        lambda p, r: og.at[p * RING + r],
        lambda p, r, k: og.at[p * RING + r, pl.ds(k * HALF, HALF), :],
        far, depth, head_send, head_receive,
        places["head_up"], places["head_down"], places["head_pair"],
    )
    heads.start(0, 1, 2, 3, 4)

    def slot(p, r, c=core):
        return r * 4 + p * 2 + c

    spread = Gather(
        lambda k: kv_ref.at[slot(near, line)]
        if k is None
        else kv_ref.at[slot(near, line), pl.ds(k * HALF, HALF), :],
        lambda p, r: kv_ref.at[slot(p, r)],
        lambda p, r, k: kv_ref.at[slot(p, r), pl.ds(k * HALF, HALF), :],
        near, line, ctx_send, ctx_receive,
        places["ctx_up"], places["ctx_down"], places["ctx_pair"],
    )
    turns = [(p, (line + d) % RING) for p in (near, 1 - near) for d in (0, 3, 1, 2)]
    passed = [
        (
            remote(
                kv_ref.at[slot(p, r)], kv_ref.at[slot(p, r)],
                sibling_send.at[k], sibling_receive.at[k], places["sibling"],
            ),
            remote(
                kv_ref.at[slot(p, r, 1 - core)], kv_ref.at[slot(p, r, 1 - core)],
                sibling_send.at[k], sibling_receive.at[k], places["sibling"],
            ),
        )
        for k, (p, r) in enumerate(turns)
    ]

    def features(p, r):
        f = p * RING + r
        return lax.dot_general(
            og[f], wo[:, pl.ds(pl.multiple_of(f * FEATURES, FEATURES), FEATURES)],
            (((1,), (1,)), ((), ())), preferred_element_type=jnp.float32,
        )

    for k in (0, 1, 2):
        local[k].wait()
    kv_ref[slot(near, line)] = jnp.dot(
        x[...], wkv[...], preferred_element_type=jnp.float32
    ).astype(jnp.bfloat16)
    local[3].wait()
    q_ref[...] = jnp.dot(x[...], wq[...], preferred_element_type=jnp.float32).astype(jnp.bfloat16)
    spread.start(0, 1, 2, 3, 4)
    passed[0][0].start()
    heads.arrive(0)
    heads.start(5)
    heads.arrive(1)
    heads.start(6)
    local[4].wait()
    local[5].wait()
    acc[...] = features(far, depth)

    before, after, opposite = (depth + 3) % RING, (depth + 1) % RING, (depth + 2) % RING
    spread.arrive(2)
    spread.start(7, 8, 9, 10)
    passed[4][0].start()
    spread.arrive(0)
    spread.start(5)
    spread.arrive(1)
    spread.start(6)
    heads.arrive(2)
    heads.start(7, 8, 9, 10)
    heads.arrive(3)
    acc[...] += features(far, before)
    heads.arrive(4)
    acc[...] += features(far, after)
    spread.arrive(3)
    passed[1][0].start()
    spread.arrive(4)
    passed[2][0].start()
    spread.arrive(7)
    spread.start(11)
    spread.arrive(8)
    spread.start(12)
    acc[...] += features(1 - far, depth)
    heads.arrive(5, 6)
    acc[...] += features(far, opposite)
    spread.arrive(5, 6)
    passed[3][0].start()
    spread.arrive(9)
    passed[5][0].start()
    spread.arrive(10)
    passed[6][0].start()
    heads.arrive(7)
    heads.start(11)
    heads.arrive(8)
    heads.start(12)
    spread.arrive(11, 12)
    passed[7][0].start()
    heads.arrive(9)
    acc[...] += features(1 - far, before)
    heads.arrive(10)
    acc[...] += features(1 - far, after)
    heads.arrive(11, 12)
    g_ref[...] = (acc[...] + features(1 - far, opposite)).astype(jnp.bfloat16)
    for sent, landed in passed:
        landed.wait_recv()
    heads.drain()
    spread.drain()
    for sent, landed in passed:
        sent.wait_send()


def front(inputs, out_grad, w_query, w_key, value_projection, w_out, peers):
    tokens, width = inputs.shape
    lanes = w_query.shape[1]
    hbm = pl.BlockSpec(memory_space=pltpu.HBM)
    vmem = pl.BlockSpec(memory_space=pltpu.VMEM)
    return pl.pallas_call(
        front_kernel,
        out_shape=(
            jax.ShapeDtypeStruct((tokens, lanes), jnp.bfloat16),
            jax.ShapeDtypeStruct((tokens, lanes), jnp.bfloat16),
            jax.ShapeDtypeStruct((peers, tokens, 2 * CHANNEL_DIM), jnp.bfloat16),
        ),
        in_specs=[hbm] * 6,
        out_specs=(vmem, vmem, vmem),
        scratch_shapes=[
            pltpu.VMEM((tokens, width), jnp.bfloat16),
            pltpu.VMEM((width, lanes), jnp.bfloat16),
            pltpu.VMEM((width, 2 * CHANNEL_DIM), jnp.bfloat16),
            pltpu.VMEM((lanes, width), jnp.bfloat16),
            pltpu.VMEM((2 * RING, tokens, FEATURES), jnp.bfloat16),
            pltpu.VMEM((tokens, lanes), jnp.float32),
            pltpu.SemaphoreType.DMA((6,)),
            pltpu.SemaphoreType.DMA((13,)),
            pltpu.SemaphoreType.DMA((13,)),
            pltpu.SemaphoreType.DMA((13,)),
            pltpu.SemaphoreType.DMA((13,)),
            pltpu.SemaphoreType.DMA((8,)),
            pltpu.SemaphoreType.DMA((8,)),
        ],
        compiler_params=pltpu.CompilerParams(
            collective_id=0, has_side_effects=True, vmem_limit_bytes=60 * 1024 * 1024
        ),
        name="front",
    )(inputs, out_grad, w_query, w_key, value_projection, w_out)


class Reduce:
    def __init__(self, held, gone, sums, ring, sends, receives, up, down):
        self.held, self.gone, self.sums = held, gone, sums
        self.before, self.after = (ring + 3) % RING, (ring + 1) % RING
        opposite = (ring + 2) % RING
        self.cut = held.shape[2] // 2
        low, high = pl.ds(0, self.cut), pl.ds(self.cut, self.cut)
        plan = [
            (held.at[opposite, :, low], gone.at[0], up),
            (held.at[opposite, :, high], gone.at[1], down),
            (held.at[self.after, :, high], sums.at[0, :, high], up),
            (held.at[self.before, :, low], sums.at[1, :, low], down),
            (held.at[self.after, :, low], sums.at[0, :, low], up),
            (held.at[self.before, :, high], sums.at[1, :, high], down),
        ]
        self.copies = [
            remote(src, dst, sends.at[k], receives.at[k], place)
            for k, (src, dst, place) in enumerate(plan)
        ]

    def start(self, *which):
        for k in which:
            self.copies[k].start()

    def relay(self):
        low, high = slice(0, self.cut), slice(self.cut, 2 * self.cut)
        for k, r, rows in ((0, self.after, low), (1, self.before, high)):
            self.copies[k].wait_recv()
            for p in range(2):
                self.held[r, p, rows] = (
                    self.held[r, p, rows].astype(jnp.float32)
                    + self.gone[k, p].astype(jnp.float32)
                ).astype(jnp.bfloat16)
            self.start(4 + k)

    def arrive(self):
        for k in (2, 3, 4, 5):
            self.copies[k].wait_recv()

    def total(self, p):
        return self.sums[0, p].astype(jnp.float32) + self.sums[1, p].astype(jnp.float32)

    def drain(self):
        for copy in self.copies:
            copy.wait_send()


def back_kernel(
    dq_ref, p_ref, wq, wk, wv,
    out_ref,
    wkv, side, held, inbox, dkv, parts, leaving, left, gone, sums, crossing, crossed,
    loads, side_send, side_receive, ctx_send, ctx_receive, head_send, head_receive,
    pair_send, pair_receive,
):
    places, (far, depth), (line, near, core) = neighbours()
    head, ctx = lax.axis_index("head"), lax.axis_index("ctx")
    others = [
        ((line + d) % RING, (near + n) % 2) for d, n in OFFSETS
    ]
    around = [(head, r * 4 + p * 2 + core) for r, p in others]
    local = [
        pltpu.make_async_copy(wk, wkv.at[:, :CHANNEL_DIM], loads.at[0]),
        pltpu.make_async_copy(wv, wkv.at[:, CHANNEL_DIM:], loads.at[1]),
    ]
    for copy in local:
        copy.start()
    greet([places["sibling"], places["head_up"], places["head_down"], places["head_pair"], *around])

    rows = p_ref.shape[4]
    swaps = [
        remote(
            p_ref.at[:, :, 1 - core, c], side.at[c],
            side_send.at[c], side_receive.at[c], places["sibling"],
        )
        for c in range(CHUNKS)
    ]
    for copy in swaps:
        copy.start()
    sends = [
        [
            remote(
                held.at[c, r, p], inbox.at[c, k],
                ctx_send.at[c, k], ctx_receive.at[c, k], around[k],
            )
            for k, (r, p) in enumerate(others)
        ]
        for c in range(CHUNKS)
    ]
    rounds = [
        Reduce(
            leaving.at[c], gone.at[c], sums.at[c], depth,
            head_send.at[c], head_receive.at[c], places["head_up"], places["head_down"],
        )
        for c in range(CHUNKS)
    ]
    across = [
        remote(
            crossing.at[c], crossed.at[c],
            pair_send.at[c], pair_receive.at[c], places["head_pair"],
        )
        for c in range(CHUNKS)
    ]

    def join(c, r, p):
        return p_ref[r, p, core, c].astype(jnp.float32) + side[c, r, p].astype(jnp.float32)

    for c in range(CHUNKS):
        swaps[c].wait_recv()
        for k, (r, p) in enumerate(others):
            held[c, r, p] = join(c, r, p).astype(jnp.bfloat16)
        for copy in sends[c]:
            copy.start()

    @pl.loop(0, 2 * RING)
    def _(f):
        parts[f] = lax.dot_general(
            dq_ref[...], wq[pl.ds(pl.multiple_of(f * FEATURES, FEATURES), FEATURES), :],
            (((1,), (1,)), ((), ())), preferred_element_type=jnp.float32,
        )

    for copy in local:
        copy.wait()

    def term(c, f):
        return parts[f, c * rows : (c + 1) * rows, :] + lax.dot_general(
            dkv[c], wkv[pl.ds(pl.multiple_of(f * FEATURES, FEATURES), FEATURES), :],
            (((1,), (1,)), ((), ())), preferred_element_type=jnp.float32,
        )

    def issue(c):
        mine = join(c, line, near)
        for k in range(len(sends[c])):
            sends[c][k].wait_recv()
            mine = mine + inbox[c, k].astype(jnp.float32)
        dkv[c] = mine.astype(jnp.bfloat16)
        for d, ready in ((2, (0, 1)), (1, (2,)), (3, (3,))):
            r = (depth + d) % RING
            for p in range(2):
                leaving[c, r, p] = term(c, p * RING + r).astype(jnp.bfloat16)
            rounds[c].start(*ready)
        for p in range(2):
            left[c, p] = term(c, p * RING + depth)

    def cross(c):
        rounds[c].arrive()
        crossing[c] = (left[c, 1 - far] + rounds[c].total(1 - far)).astype(jnp.bfloat16)
        across[c].start()
        left[c, far] = left[c, far] + rounds[c].total(far)

    issue(0)
    for c in range(1, CHUNKS):
        issue(c)
        rounds[c - 1].relay()
        if c > 1:
            cross(c - 2)
    rounds[CHUNKS - 1].relay()
    cross(CHUNKS - 2)
    cross(CHUNKS - 1)
    for c in range(CHUNKS):
        across[c].wait_recv()
        out_ref[c * rows : (c + 1) * rows, :] = (
            left[c, far] + crossed[c].astype(jnp.float32)
        ).astype(jnp.bfloat16)
    for c in range(CHUNKS):
        swaps[c].wait_send()
        across[c].wait_send()
        rounds[c].drain()
        for copy in sends[c]:
            copy.wait_send()


def back(query_grad, pieces, w_query, w_key, value_projection):
    tokens, lanes = query_grad.shape
    width = w_query.shape[0]
    rows = tokens // CHUNKS
    vmem = pl.BlockSpec(memory_space=pltpu.VMEM)
    wide = 2 * CHANNEL_DIM
    bf16, f32 = jnp.bfloat16, jnp.float32
    dma = pltpu.SemaphoreType.DMA
    return pl.pallas_call(
        back_kernel,
        out_shape=jax.ShapeDtypeStruct((tokens, FEATURES), bf16),
        in_specs=[vmem] * 5,
        out_specs=vmem,
        scratch_shapes=[
            pltpu.VMEM((width, wide), bf16),
            pltpu.VMEM((CHUNKS, RING, 2, rows, wide), bf16),
            pltpu.VMEM((CHUNKS, RING, 2, rows, wide), bf16),
            pltpu.VMEM((CHUNKS, len(OFFSETS), rows, wide), bf16),
            pltpu.VMEM((CHUNKS, rows, wide), bf16),
            pltpu.VMEM((2 * RING, tokens, FEATURES), f32),
            pltpu.VMEM((CHUNKS, RING, 2, rows, FEATURES), bf16),
            pltpu.VMEM((CHUNKS, 2, rows, FEATURES), f32),
            pltpu.VMEM((CHUNKS, 2, 2, rows // 2, FEATURES), bf16),
            pltpu.VMEM((CHUNKS, 2, 2, rows, FEATURES), bf16),
            pltpu.VMEM((CHUNKS, rows, FEATURES), bf16),
            pltpu.VMEM((CHUNKS, rows, FEATURES), bf16),
            dma((2,)),
            dma((CHUNKS,)),
            dma((CHUNKS,)),
            dma((CHUNKS, len(OFFSETS))),
            dma((CHUNKS, len(OFFSETS))),
            dma((CHUNKS, 6)),
            dma((CHUNKS, 6)),
            dma((CHUNKS,)),
            dma((CHUNKS,)),
        ],
        compiler_params=pltpu.CompilerParams(
            collective_id=1, has_side_effects=True, vmem_limit_bytes=32 * 1024 * 1024
        ),
        name="back",
    )(query_grad, pieces, w_query, w_key, value_projection)


def attention_kernel(
    span_ref, length_ref, q_ref, g_ref, kv_ref,
    dq_ref, dkv_ref,
    kvs, qs, gs, s_buf, d_buf, acc, dqt,
):
    exponent = LOG2E / math.sqrt(CHANNEL_DIM)
    scale = 1.0 / math.sqrt(CHANNEL_DIM)
    spans = span_ref.shape[0]

    @pl.loop(0, spans)
    def _(r):
        p = span_ref[r]
        kvs[pl.ds(pl.multiple_of(p * HALF, HALF), HALF), :] = kv_ref[
            pl.ds(pl.multiple_of(r * HALF, HALF), HALF), :
        ]
        acc[pl.ds(pl.multiple_of(r * HALF, HALF), HALF), :] = jnp.zeros((HALF, 2 * CHANNEL_DIM), jnp.float32)

    lanes = BUNDLE * HALF
    for b in range(2):
        rows = slice(b * HALF, (b + 1) * HALF)
        for h in range(BUNDLE):
            cols = slice(h * CHANNEL_DIM, (h + 1) * CHANNEL_DIM)
            qs[h * HALF : (h + 1) * HALF, :] = q_ref[rows, cols]
            gs[h * HALF : (h + 1) * HALF, :] = g_ref[rows, cols]
        c = span_ref[2 * lax.axis_index("ctx") + b]
        position = c * HALF + lax.broadcasted_iota(jnp.int32, (1, HALF), 1)
        start = jnp.zeros((1, HALF), jnp.int32)
        first = 0
        end = 0
        for k in range(length_ref.shape[0]):
            end = end + length_ref[k]
            start = jnp.where(position >= end, end, start)
            first = jnp.where(c * HALF >= end, end, first)
        low = first // TILE
        high = c // (TILE // HALF) + 1

        def gather_stats(t, carry):
            top, total, inner = carry
            at = pl.ds(pl.multiple_of(t * TILE, TILE), TILE)
            keys = kvs[at, :CHANNEL_DIM]
            values = kvs[at, CHANNEL_DIM:]
            key_position = t * TILE + lax.broadcasted_iota(jnp.int32, (TILE, HALF), 0)
            bias = jnp.where(
                (key_position <= position) & (key_position >= start), 0.0, MASKED
            )
            bias = jnp.concatenate([bias] * BUNDLE, axis=1)
            s = lax.dot_general(
                keys, qs[...], (((1,), (1,)), ((), ())), preferred_element_type=jnp.float32
            )
            s = s * exponent + bias
            s_buf[at, :] = s
            fresh = jnp.maximum(top, jnp.max(s, axis=0, keepdims=True))
            factor = jnp.exp2(top - fresh)
            e = jnp.exp2(s - fresh)
            slopes = lax.dot_general(
                values, gs[...], (((1,), (1,)), ((), ())), preferred_element_type=jnp.float32
            )
            d_buf[at, :] = slopes
            total = total * factor + jnp.sum(e, axis=0, keepdims=True)
            inner = inner * factor + jnp.sum(e * slopes, axis=0, keepdims=True)
            return fresh, total, inner

        zero = jnp.zeros((1, lanes), jnp.float32)
        top, total, inner = lax.fori_loop(
            low, high, gather_stats, (jnp.full((1, lanes), MASKED, jnp.float32), zero, zero)
        )
        delta = inner / total
        level = top + jnp.log2(total)
        dqt[...] = jnp.zeros_like(dqt)

        @pl.loop(low, high)
        def _(t):
            at = pl.ds(pl.multiple_of(t * TILE, TILE), TILE)
            probability = jnp.exp2(s_buf[at, :] - level)
            score_grad = (probability * (d_buf[at, :] - delta)).astype(jnp.bfloat16)
            rounded = probability.astype(jnp.bfloat16)
            acc[at, CHANNEL_DIM:] += jnp.dot(rounded, gs[...], preferred_element_type=jnp.float32)
            acc[at, :CHANNEL_DIM] += jnp.dot(score_grad, qs[...], preferred_element_type=jnp.float32)
            dqt[...] += lax.dot_general(
                kvs[at, :CHANNEL_DIM], score_grad, (((0,), (0,)), ((), ())),
                preferred_element_type=jnp.float32,
            )

        for h in range(BUNDLE):
            dq_ref[rows, h * CHANNEL_DIM : (h + 1) * CHANNEL_DIM] = (
                (dqt[:, h * HALF : (h + 1) * HALF] * scale).T.astype(jnp.bfloat16)
            )

    @pl.loop(0, spans)
    def _(r):
        p = span_ref[r]
        at = pl.ds(pl.multiple_of(p * HALF, HALF), HALF)
        to = pl.ds(pl.multiple_of(r * HALF, HALF), HALF)
        dkv_ref[to, :CHANNEL_DIM] = (acc[at, :CHANNEL_DIM] * scale).astype(jnp.bfloat16)
        dkv_ref[to, CHANNEL_DIM:] = acc[at, CHANNEL_DIM:].astype(jnp.bfloat16)


def attention(q, g, kv, span_order, doc_lengths):
    tokens = q.shape[0]
    length = kv.shape[0]
    smem = pl.BlockSpec(memory_space=pltpu.SMEM)
    vmem = pl.BlockSpec(memory_space=pltpu.VMEM)
    lanes = BUNDLE * HALF
    return pl.pallas_call(
        attention_kernel,
        out_shape=(
            jax.ShapeDtypeStruct((tokens, lanes), jnp.bfloat16),
            jax.ShapeDtypeStruct((length, 2 * CHANNEL_DIM), jnp.bfloat16),
        ),
        in_specs=[smem, smem, vmem, vmem, vmem],
        out_specs=(vmem, vmem),
        scratch_shapes=[
            pltpu.VMEM((length, 2 * CHANNEL_DIM), jnp.bfloat16),
            pltpu.VMEM((lanes, CHANNEL_DIM), jnp.bfloat16),
            pltpu.VMEM((lanes, CHANNEL_DIM), jnp.bfloat16),
            pltpu.VMEM((length, lanes), jnp.float32),
            pltpu.VMEM((length, lanes), jnp.float32),
            pltpu.VMEM((length, 2 * CHANNEL_DIM), jnp.float32),
            pltpu.VMEM((CHANNEL_DIM, lanes), jnp.float32),
        ],
        compiler_params=pltpu.CompilerParams(vmem_limit_bytes=40 * 1024 * 1024),
        name="attention",
    )(span_order, doc_lengths, q, g, kv)


def shards(inputs, out_grad, w_query, w_key, value_projection, w_out, doc_lengths, span_order):
    tokens = inputs.shape[0]
    peers = lax.axis_size("ctx")
    query, context_grad, gathered = front(
        inputs, out_grad, w_query, w_key, value_projection, w_out, peers
    )
    query_grad, pieces = attention(
        query, context_grad, gathered.reshape(peers * tokens, -1), span_order, doc_lengths
    )
    pieces = pieces.reshape(RING, 2, 2, CHUNKS, tokens // CHUNKS, -1)
    return back(query_grad, pieces, w_query, w_key, value_projection)


def solution(mesh):
    in_specs = (
        P("ctx", None),
        P("ctx", "head"),
        P(None, "head"),
        P(None, "head"),
        P(None, "head"),
        P("head", None),
        P(),
        P(),
    )
    return jax.shard_map(
        shards, mesh=mesh, in_specs=in_specs, out_specs=P("ctx", "head"), check_vma=False
    )
```

profile of v0, /device:TPU:1, one launch (start us, length us, event | category | flops | bytes accessed | tf_op | source)
XLA Modules:
  0.0 79.2 jit_solution(12260238783790306834)
XLA Ops:
  0.0 0.0 copy-start.6
  0.0 0.0 copy-start.7
  0.0 28.1 %front.1 = (bf16[256,512]{1,0:T(8,128)(2,1)}, bf16[256,512]{1,0:T(8,128)(2,1)}, bf16[16,256,256]{2,1,0:T(8,128)(2,1)}) custom-call(bf16[256,4096]{1,0:T(8,128)(2,1)} %x_hbm.1, bf16[256,512]{1,0:T(8,128)(2,1)} %og_hbm.1, bf16[4096,512]{1,0:T(8,128)(2,1)} %wq.1, bf16[4096,128]{1,0:T(8,128)(2,1)} %wk.1, bf16[4096,128]{1,0:T(8,128)(2,1)} %wv.1, ...), custom_call_target="tpu_custom_call" | custom-call | tf_op jit(solution)/shard_map/front/pallas_call | solution.py:241
  28.1 0.0 copy-start.1
  28.2 0.0 copy-start.2
  28.2 0.0 copy-done.6
  28.2 0.0 copy-done.7
  28.2 0.0 copy-start.3
  28.2 1.7 %copy-done.3 = bf16[16,256,256]{2,1,0:T(8,128)(2,1)S(1)} copy-done((bf16[16,256,256]{2,1,0:T(8,128)(2,1)S(1)}, bf16[16,256,256]{2,1,0:T(8,128)(2,1)}, u32[]{:S(2)}) %copy-start.3) | copy-done | bytes 2097176
  29.9 0.0 copy-start.4
  29.9 0.9 %copy-done.4 = bf16[256,512]{1,0:T(8,128)(2,1)S(1)} copy-done((bf16[256,512]{1,0:T(8,128)(2,1)S(1)}, bf16[256,512]{1,0:T(8,128)(2,1)}, u32[]{:S(2)}) %copy-start.4) | copy-done | bytes 262168
  30.9 0.0 copy-start.5
  30.9 0.9 %copy-done.5 = bf16[256,512]{1,0:T(8,128)(2,1)S(1)} copy-done((bf16[256,512]{1,0:T(8,128)(2,1)S(1)}, bf16[256,512]{1,0:T(8,128)(2,1)}, u32[]{:S(2)}) %copy-start.5) | copy-done | bytes 262168
  31.8 6.0 %attention.1 = (bf16[256,512]{1,0:T(8,128)(2,1)S(1)}, bf16[4096,256]{1,0:T(8,128)(2,1)S(1)}) custom-call(s32[32]{0:T(128)S(1)} %copy-done.6, s32[8]{0:T(128)S(1)} %copy-done.7, bf16[256,512]{1,0:T(8,128)(2,1)S(1)} %copy-done.4, bf16[256,512]{1,0:T(8,128)(2,1)S(1)} %copy-done.5, bf16[4096,256]{1,0:T(8,128)(2,1)S(1)} %bitcast.3), custom_call_target="tpu_custom_call" | custom-call | tf_op jit(solution)/shard_map/attention/pallas_call | solution.py:589
  37.8 0.0 copy-done.1
  37.9 0.0 copy-done.2
  37.9 0.0 copy-start
  37.9 2.2 %copy-done = bf16[4096,512]{1,0:T(8,128)(2,1)S(1)} copy-done((bf16[4096,512]{1,0:T(8,128)(2,1)S(1)}, bf16[4096,512]{1,0:T(8,128)(2,1)}, u32[]{:S(2)}) %copy-start) | copy-done | bytes 4194328
  40.1 38.4 %back.1 = bf16[256,512]{1,0:T(8,128)(2,1)S(1)} custom-call(bf16[256,512]{1,0:T(8,128)(2,1)S(1)} %get-tuple-element.13.dq_ref, bf16[4,2,2,4,64,256]{5,4,3,2,1,0:T(8,128)(2,1)S(1)} %bitcast.2, bf16[4096,512]{1,0:T(8,128)(2,1)S(1)} %copy-done, bf16[4096,128]{1,0:T(8,128)(2,1)S(1)} %copy-done.1, bf16[4096,128]{1,0:T(8,128)(2,1)S(1)} %copy-done.2), custom_call_target="tpu_custom_call" | custom-call | tf_op jit(solution)/shard_map/back/pallas_call | solution.py:451
  78.5 0.7 copy.10
Async XLA Ops:
  0.0 28.2 %copy-start.6 = (s32[32]{0:T(128)S(1)}, s32[32]{0:T(128)}, u32[]{:S(2)}) copy-start(s32[32]{0:T(128)} %span_ref.1) | copy-start | bytes 388
  0.0 28.2 %copy-start.7 = (s32[8]{0:T(128)S(1)}, s32[8]{0:T(128)}, u32[]{:S(2)}) copy-start(s32[8]{0:T(128)} %length_ref.1) | copy-start | bytes 100
  28.1 9.7 %copy-start.1 = (bf16[4096,128]{1,0:T(8,128)(2,1)S(1)}, bf16[4096,128]{1,0:T(8,128)(2,1)}, u32[]{:S(2)}) copy-start(bf16[4096,128]{1,0:T(8,128)(2,1)} %wk.1) | copy-start | bytes 3145732
  28.2 9.7 %copy-start.2 = (bf16[4096,128]{1,0:T(8,128)(2,1)S(1)}, bf16[4096,128]{1,0:T(8,128)(2,1)}, u32[]{:S(2)}) copy-start(bf16[4096,128]{1,0:T(8,128)(2,1)} %wv.1) | copy-start | bytes 3145732
  28.2 1.7 %copy-start.3 = (bf16[16,256,256]{2,1,0:T(8,128)(2,1)S(1)}, bf16[16,256,256]{2,1,0:T(8,128)(2,1)}, u32[]{:S(2)}) copy-start(bf16[16,256,256]{2,1,0:T(8,128)(2,1)} %get-tuple-element.12) | copy-start | bytes 6291460
  29.9 0.9 %copy-start.4 = (bf16[256,512]{1,0:T(8,128)(2,1)S(1)}, bf16[256,512]{1,0:T(8,128)(2,1)}, u32[]{:S(2)}) copy-start(bf16[256,512]{1,0:T(8,128)(2,1)} %get-tuple-element.10.q_ref) | copy-start | bytes 786436
  30.9 0.9 %copy-start.5 = (bf16[256,512]{1,0:T(8,128)(2,1)S(1)}, bf16[256,512]{1,0:T(8,128)(2,1)}, u32[]{:S(2)}) copy-start(bf16[256,512]{1,0:T(8,128)(2,1)} %get-tuple-element.11.g_ref) | copy-start | bytes 786436
  37.9 2.2 %copy-start = (bf16[4096,512]{1,0:T(8,128)(2,1)S(1)}, bf16[4096,512]{1,0:T(8,128)(2,1)}, u32[]{:S(2)}) copy-start(bf16[4096,512]{1,0:T(8,128)(2,1)} %wq.1) | copy-start | bytes 12582916
where the time goes:
time: 79.4 us; the launch traced here: 79.2 us
  Pallas kernels  72.6 us (91%)
  local copies, waits for them, and re-layouts  6.53 us (8%)
    pallas_call x1, Pallas kernels, back(): pl.pallas_call(back_kernel, out_shape=jax.ShapeDtypeStruct((tokens, FEATU...  38.4 us
    pallas_call x1, Pallas kernels, front(): pl.pallas_call(front_kernel, out_shape=(jax.ShapeDtypeStruct((tokens, lan...  28.1 us
    unnamed x17, local copies, waits for them, and re-layouts  6.53 us
    pallas_call x1, Pallas kernels, attention(): pl.pallas_call(attention_kernel, out_shape=(jax.ShapeDtypeStruct((tokens,...  6.01 us

commit v1 on v0

--- a/solution.py
+++ b/solution.py
@@ -19,6 +19,7 @@
 OFFSETS = ((2, 1), (2, 0), (1, 1), (3, 1), (1, 0), (3, 0), (0, 1))
 LOG2E = 1.4426950408889634
 MASKED = -1e30
+GRANT = 60 * 1024 * 1024
 MESH = pl.DeviceIdType.MESH
 
 
@@ -104,9 +105,9 @@
 
 def front_kernel(
     x_hbm, og_hbm, wq_hbm, wk_hbm, wv_hbm, wo_hbm,
-    q_ref, g_ref, kv_ref,
-    x, wq, wkv, wo, og, acc,
-    loads, head_send, head_receive, ctx_send, ctx_receive, sibling_send, sibling_receive,
+    q_hbm, g_hbm, kv_hbm,
+    x, wq, wkv, wo, og, acc, q_ref, g_ref, kv_ref,
+    loads, stores, head_send, head_receive, ctx_send, ctx_receive, sibling_send, sibling_receive,
 ):
     places, (far, depth), (line, near, core) = neighbours()
     me = far * RING + depth
@@ -120,6 +121,11 @@
     ]
     for copy in local:
         copy.start()
+    saved = [
+        pltpu.make_async_copy(q_ref, q_hbm, stores.at[0]),
+        pltpu.make_async_copy(kv_ref, kv_hbm, stores.at[1]),
+        pltpu.make_async_copy(g_ref, g_hbm, stores.at[2]),
+    ]
     greet(list(places.values()))
 
     heads = Gather(
@@ -174,6 +180,7 @@
     q_ref[...] = jnp.dot(x[...], wq[...], preferred_element_type=jnp.float32).astype(jnp.bfloat16)
     spread.start(0, 1, 2, 3, 4)
     passed[0][0].start()
+    saved[0].start()
     heads.arrive(0)
     heads.start(5)
     heads.arrive(1)
@@ -223,21 +230,24 @@
     acc[...] += features(1 - far, before)
     heads.arrive(10)
     acc[...] += features(1 - far, after)
+    for sent, landed in passed:
+        landed.wait_recv()
+    saved[1].start()
     heads.arrive(11, 12)
     g_ref[...] = (acc[...] + features(1 - far, opposite)).astype(jnp.bfloat16)
-    for sent, landed in passed:
-        landed.wait_recv()
+    saved[2].start()
     heads.drain()
     spread.drain()
     for sent, landed in passed:
         sent.wait_send()
+    for copy in saved:
+        copy.wait()
 
 
 def front(inputs, out_grad, w_query, w_key, value_projection, w_out, peers):
     tokens, width = inputs.shape
     lanes = w_query.shape[1]
-    hbm = pl.BlockSpec(memory_space=pltpu.HBM)
-    vmem = pl.BlockSpec(memory_space=pltpu.VMEM)
+    hbm = pl.BlockSpec(memory_space=pl.ANY)
     return pl.pallas_call(
         front_kernel,
         out_shape=(
@@ -246,7 +256,7 @@
             jax.ShapeDtypeStruct((peers, tokens, 2 * CHANNEL_DIM), jnp.bfloat16),
         ),
         in_specs=[hbm] * 6,
-        out_specs=(vmem, vmem, vmem),
+        out_specs=(hbm, hbm, hbm),
         scratch_shapes=[
             pltpu.VMEM((tokens, width), jnp.bfloat16),
             pltpu.VMEM((width, lanes), jnp.bfloat16),
@@ -254,7 +264,11 @@
             pltpu.VMEM((lanes, width), jnp.bfloat16),
             pltpu.VMEM((2 * RING, tokens, FEATURES), jnp.bfloat16),
             pltpu.VMEM((tokens, lanes), jnp.float32),
+            pltpu.VMEM((tokens, lanes), jnp.bfloat16),
+            pltpu.VMEM((tokens, lanes), jnp.bfloat16),
+            pltpu.VMEM((peers, tokens, 2 * CHANNEL_DIM), jnp.bfloat16),
             pltpu.SemaphoreType.DMA((6,)),
+            pltpu.SemaphoreType.DMA((3,)),
             pltpu.SemaphoreType.DMA((13,)),
             pltpu.SemaphoreType.DMA((13,)),
             pltpu.SemaphoreType.DMA((13,)),
@@ -263,7 +277,7 @@
             pltpu.SemaphoreType.DMA((8,)),
         ],
         compiler_params=pltpu.CompilerParams(
-            collective_id=0, has_side_effects=True, vmem_limit_bytes=60 * 1024 * 1024
+            collective_id=0, has_side_effects=True, vmem_limit_bytes=GRANT
         ),
         name="front",
     )(inputs, out_grad, w_query, w_key, value_projection, w_out)
@@ -317,9 +331,9 @@
 
 
 def back_kernel(
-    dq_ref, p_ref, wq, wk, wv,
+    dq_hbm, p_hbm, wq_hbm, wk_hbm, wv_hbm,
     out_ref,
-    wkv, side, held, inbox, dkv, parts, leaving, left, gone, sums, crossing, crossed,
+    dq, mine, wq, wkv, side, held, inbox, dkv, parts, leaving, left, gone, sums, crossing, crossed,
     loads, side_send, side_receive, ctx_send, ctx_receive, head_send, head_receive,
     pair_send, pair_receive,
 ):
@@ -330,17 +344,20 @@
     ]
     around = [(head, r * 4 + p * 2 + core) for r, p in others]
     local = [
-        pltpu.make_async_copy(wk, wkv.at[:, :CHANNEL_DIM], loads.at[0]),
-        pltpu.make_async_copy(wv, wkv.at[:, CHANNEL_DIM:], loads.at[1]),
+        pltpu.make_async_copy(p_hbm.at[:, :, core], mine, loads.at[0]),
+        pltpu.make_async_copy(dq_hbm, dq, loads.at[1]),
+        pltpu.make_async_copy(wq_hbm, wq, loads.at[2]),
+        pltpu.make_async_copy(wk_hbm, wkv.at[:, :CHANNEL_DIM], loads.at[3]),
+        pltpu.make_async_copy(wv_hbm, wkv.at[:, CHANNEL_DIM:], loads.at[4]),
     ]
     for copy in local:
         copy.start()
     greet([places["sibling"], places["head_up"], places["head_down"], places["head_pair"], *around])
 
-    rows = p_ref.shape[4]
+    rows = mine.shape[3]
     swaps = [
         remote(
-            p_ref.at[:, :, 1 - core, c], side.at[c],
+            p_hbm.at[:, :, 1 - core, c], side.at[c],
             side_send.at[c], side_receive.at[c], places["sibling"],
         )
         for c in range(CHUNKS)
@@ -373,8 +390,9 @@
     ]
 
     def join(c, r, p):
-        return p_ref[r, p, core, c].astype(jnp.float32) + side[c, r, p].astype(jnp.float32)
-
+        return mine[r, p, c].astype(jnp.float32) + side[c, r, p].astype(jnp.float32)
+
+    local[0].wait()
     for c in range(CHUNKS):
         swaps[c].wait_recv()
         for k, (r, p) in enumerate(others):
@@ -382,15 +400,18 @@
         for copy in sends[c]:
             copy.start()
 
+    local[1].wait()
+    local[2].wait()
+
     @pl.loop(0, 2 * RING)
     def _(f):
         parts[f] = lax.dot_general(
-            dq_ref[...], wq[pl.ds(pl.multiple_of(f * FEATURES, FEATURES), FEATURES), :],
+            dq[...], wq[pl.ds(pl.multiple_of(f * FEATURES, FEATURES), FEATURES), :],
             (((1,), (1,)), ((), ())), preferred_element_type=jnp.float32,
         )
 
-    for copy in local:
-        copy.wait()
+    local[3].wait()
+    local[4].wait()
 
     def term(c, f):
         return parts[f, c * rows : (c + 1) * rows, :] + lax.dot_general(
@@ -399,11 +420,11 @@
         )
 
     def issue(c):
-        mine = join(c, line, near)
+        total = join(c, line, near)
         for k in range(len(sends[c])):
             sends[c][k].wait_recv()
-            mine = mine + inbox[c, k].astype(jnp.float32)
-        dkv[c] = mine.astype(jnp.bfloat16)
+            total = total + inbox[c, k].astype(jnp.float32)
+        dkv[c] = total.astype(jnp.bfloat16)
         for d, ready in ((2, (0, 1)), (1, (2,)), (3, (3,))):
             r = (depth + d) % RING
             for p in range(2):
@@ -445,15 +466,19 @@
     width = w_query.shape[0]
     rows = tokens // CHUNKS
     vmem = pl.BlockSpec(memory_space=pltpu.VMEM)
+    hbm = pl.BlockSpec(memory_space=pl.ANY)
     wide = 2 * CHANNEL_DIM
     bf16, f32 = jnp.bfloat16, jnp.float32
     dma = pltpu.SemaphoreType.DMA
     return pl.pallas_call(
         back_kernel,
         out_shape=jax.ShapeDtypeStruct((tokens, FEATURES), bf16),
-        in_specs=[vmem] * 5,
+        in_specs=[hbm] * 5,
         out_specs=vmem,
         scratch_shapes=[
+            pltpu.VMEM((tokens, lanes), bf16),
+            pltpu.VMEM((RING, 2, CHUNKS, rows, wide), bf16),
+            pltpu.VMEM((width, lanes), bf16),
             pltpu.VMEM((width, wide), bf16),
             pltpu.VMEM((CHUNKS, RING, 2, rows, wide), bf16),
             pltpu.VMEM((CHUNKS, RING, 2, rows, wide), bf16),
@@ -466,7 +491,7 @@
             pltpu.VMEM((CHUNKS, 2, 2, rows, FEATURES), bf16),
             pltpu.VMEM((CHUNKS, rows, FEATURES), bf16),
             pltpu.VMEM((CHUNKS, rows, FEATURES), bf16),
-            dma((2,)),
+            dma((5,)),
             dma((CHUNKS,)),
             dma((CHUNKS,)),
             dma((CHUNKS, len(OFFSETS))),
@@ -477,29 +502,45 @@
             dma((CHUNKS,)),
         ],
         compiler_params=pltpu.CompilerParams(
-            collective_id=1, has_side_effects=True, vmem_limit_bytes=32 * 1024 * 1024
+            collective_id=1, has_side_effects=True, vmem_limit_bytes=GRANT
         ),
         name="back",
     )(query_grad, pieces, w_query, w_key, value_projection)
 
 
 def attention_kernel(
-    span_ref, length_ref, q_ref, g_ref, kv_ref,
-    dq_ref, dkv_ref,
-    kvs, qs, gs, s_buf, d_buf, acc, dqt,
+    span_ref, length_ref, q_hbm, g_hbm, kv_hbm,
+    dq_hbm, dkv_hbm,
+    kvs, qs, gs, s_buf, d_buf, acc, dqt, q_ref, g_ref, dq_ref, dkv_ref,
+    loads, stores,
 ):
     exponent = LOG2E / math.sqrt(CHANNEL_DIM)
     scale = 1.0 / math.sqrt(CHANNEL_DIM)
     spans = span_ref.shape[0]
 
+    local = [
+        pltpu.make_async_copy(q_hbm, q_ref, loads.at[0]),
+        pltpu.make_async_copy(g_hbm, g_ref, loads.at[1]),
+    ]
+    for copy in local:
+        copy.start()
+
     @pl.loop(0, spans)
     def _(r):
         p = span_ref[r]
-        kvs[pl.ds(pl.multiple_of(p * HALF, HALF), HALF), :] = kv_ref[
-            pl.ds(pl.multiple_of(r * HALF, HALF), HALF), :
-        ]
+        pltpu.make_async_copy(
+            kv_hbm.at[pl.ds(pl.multiple_of(r * HALF, HALF), HALF), :],
+            kvs.at[pl.ds(pl.multiple_of(p * HALF, HALF), HALF), :],
+            loads.at[2],
+        ).start()
+
+    @pl.loop(0, spans)
+    def _(r):
         acc[pl.ds(pl.multiple_of(r * HALF, HALF), HALF), :] = jnp.zeros((HALF, 2 * CHANNEL_DIM), jnp.float32)
 
+    for copy in local:
+        copy.wait()
+    pltpu.make_async_copy(kv_hbm, kvs, loads.at[2]).wait()
     lanes = BUNDLE * HALF
     for b in range(2):
         rows = slice(b * HALF, (b + 1) * HALF)
@@ -571,6 +612,9 @@
                 (dqt[:, h * HALF : (h + 1) * HALF] * scale).T.astype(jnp.bfloat16)
             )
 
+    grads = pltpu.make_async_copy(dq_ref, dq_hbm, stores.at[0])
+    grads.start()
+
     @pl.loop(0, spans)
     def _(r):
         p = span_ref[r]
@@ -578,13 +622,17 @@
         to = pl.ds(pl.multiple_of(r * HALF, HALF), HALF)
         dkv_ref[to, :CHANNEL_DIM] = (acc[at, :CHANNEL_DIM] * scale).astype(jnp.bfloat16)
         dkv_ref[to, CHANNEL_DIM:] = acc[at, CHANNEL_DIM:].astype(jnp.bfloat16)
+        pltpu.make_async_copy(dkv_ref.at[to, :], dkv_hbm.at[to, :], stores.at[1]).start()
+
+    grads.wait()
+    pltpu.make_async_copy(dkv_ref, dkv_hbm, stores.at[1]).wait()
 
 
 def attention(q, g, kv, span_order, doc_lengths):
     tokens = q.shape[0]
     length = kv.shape[0]
     smem = pl.BlockSpec(memory_space=pltpu.SMEM)
-    vmem = pl.BlockSpec(memory_space=pltpu.VMEM)
+    hbm = pl.BlockSpec(memory_space=pl.ANY)
     lanes = BUNDLE * HALF
     return pl.pallas_call(
         attention_kernel,
@@ -592,8 +640,8 @@
             jax.ShapeDtypeStruct((tokens, lanes), jnp.bfloat16),
             jax.ShapeDtypeStruct((length, 2 * CHANNEL_DIM), jnp.bfloat16),
         ),
-        in_specs=[smem, smem, vmem, vmem, vmem],
-        out_specs=(vmem, vmem),
+        in_specs=[smem, smem, hbm, hbm, hbm],
+        out_specs=(hbm, hbm),
         scratch_shapes=[
             pltpu.VMEM((length, 2 * CHANNEL_DIM), jnp.bfloat16),
             pltpu.VMEM((lanes, CHANNEL_DIM), jnp.bfloat16),
@@ -602,8 +650,14 @@
             pltpu.VMEM((length, lanes), jnp.float32),
             pltpu.VMEM((length, 2 * CHANNEL_DIM), jnp.float32),
             pltpu.VMEM((CHANNEL_DIM, lanes), jnp.float32),
+            pltpu.VMEM((tokens, lanes), jnp.bfloat16),
+            pltpu.VMEM((tokens, lanes), jnp.bfloat16),
+            pltpu.VMEM((tokens, lanes), jnp.bfloat16),
+            pltpu.VMEM((length, 2 * CHANNEL_DIM), jnp.bfloat16),
+            pltpu.SemaphoreType.DMA((3,)),
+            pltpu.SemaphoreType.DMA((2,)),
         ],
-        compiler_params=pltpu.CompilerParams(vmem_limit_bytes=40 * 1024 * 1024),
+        compiler_params=pltpu.CompilerParams(vmem_limit_bytes=GRANT),
         name="attention",
     )(span_order, doc_lengths, q, g, kv)
 

time: 79.4 us -> 76.7 us (0.966)
  local copies, waits for them, and re-layouts: 6.53 us -> 1.67 us
  Pallas kernels: 72.6 us -> 74.8 us
    unnamed x17 -> x1, local copies, waits for them, and re-layouts: 6.53 us -> 1.67 us
    pallas_call x1, Pallas kernels: 6.01 us -> 8.09 us  [attention(): pl.pallas_call(attention_kernel, out_shape=(jax.ShapeDtypeStruct((tokens,...]
where the time goes in v1:
time: 76.7 us; the launch traced here: 76.5 us
  Pallas kernels  74.8 us (98%)
  local copies, waits for them, and re-layouts  1.67 us (2%)
    pallas_call x1, Pallas kernels, back(): pl.pallas_call(back_kernel, out_shape=jax.ShapeDtypeStruct((tokens, FEATU...  38.8 us
    pallas_call x1, Pallas kernels, front(): pl.pallas_call(front_kernel, out_shape=(jax.ShapeDtypeStruct((tokens, lan...  27.9 us
    pallas_call x1, Pallas kernels, attention(): pl.pallas_call(attention_kernel, out_shape=(jax.ShapeDtypeStruct((tokens,...  8.09 us
    unnamed x1, local copies, waits for them, and re-layouts  1.67 us

profile of v1, /device:TPU:1, one launch (start us, length us, event | category | flops | bytes accessed | tf_op | source)
XLA Modules:
  0.0 76.5 jit_solution(9401675428523586875)
XLA Ops:
  0.0 27.9 %front.1 = (bf16[256,512]{1,0:T(8,128)(2,1)}, bf16[256,512]{1,0:T(8,128)(2,1)}, bf16[16,256,256]{2,1,0:T(8,128)(2,1)}) custom-call(bf16[256,4096]{1,0:T(8,128)(2,1)} %x_hbm.1, bf16[256,512]{1,0:T(8,128)(2,1)} %og_hbm.1, bf16[4096,512]{1,0:T(8,128)(2,1)} %wq_hbm.3, bf16[4096,128]{1,0:T(8,128)(2,1)} %wk_hbm.3, bf16[4096,128]{1,0:T(8,128)(2,1)} %wv_hbm.3, ...), custom_call_target="tpu_custom_call" | custom-call | tf_op jit(solution)/shard_map/front/pallas_call | solution.py:251
  27.9 8.1 %attention.1 = (bf16[256,512]{1,0:T(8,128)(2,1)}, bf16[4096,256]{1,0:T(8,128)(2,1)}) custom-call(s32[32]{0:T(128)} %span_ref.1, s32[8]{0:T(128)} %length_ref.1, bf16[256,512]{1,0:T(8,128)(2,1)} %get-tuple-element.10.q_hbm, bf16[256,512]{1,0:T(8,128)(2,1)} %get-tuple-element.11.g_hbm, bf16[4096,256]{1,0:T(8,128)(2,1)} %bitcast.3), custom_call_target="tpu_custom_call" | custom-call | tf_op jit(solution)/shard_map/attention/pallas_call | solution.py:637
  36.0 38.8 %back.1 = bf16[256,512]{1,0:T(8,128)(2,1)} custom-call(bf16[256,512]{1,0:T(8,128)(2,1)} %get-tuple-element.13.dq_hbm, bf16[4,2,2,4,64,256]{5,4,3,2,1,0:T(8,128)(2,1)} %bitcast.2, bf16[4096,512]{1,0:T(8,128)(2,1)} %wq_hbm.3, bf16[4096,128]{1,0:T(8,128)(2,1)} %wk_hbm.3, bf16[4096,128]{1,0:T(8,128)(2,1)} %wv_hbm.3), custom_call_target="tpu_custom_call" | custom-call | tf_op jit(solution)/shard_map/back/pallas_call | solution.py:473
  74.8 1.7 %copy.10 = bf16[256,512]{1,0:T(8,128)(2,1)} copy(bf16[256,512]{1,0:T(8,128)(2,1)} %back.1) | data formatting | bytes 524288

commit v2 on v1

--- a/solution.py
+++ b/solution.py
@@ -331,7 +331,7 @@
 
 
 def back_kernel(
-    dq_hbm, p_hbm, wq_hbm, wk_hbm, wv_hbm,
+    p_hbm, wq_hbm, wk_hbm, wv_hbm,
     out_ref,
     dq, mine, wq, wkv, side, held, inbox, dkv, parts, leaving, left, gone, sums, crossing, crossed,
     loads, side_send, side_receive, ctx_send, ctx_receive, head_send, head_receive,
@@ -344,8 +344,8 @@
     ]
     around = [(head, r * 4 + p * 2 + core) for r, p in others]
     local = [
-        pltpu.make_async_copy(p_hbm.at[:, :, core], mine, loads.at[0]),
-        pltpu.make_async_copy(dq_hbm, dq, loads.at[1]),
+        pltpu.make_async_copy(p_hbm.at[pl.ds(1, 2 * RING), core], mine, loads.at[0]),
+        pltpu.make_async_copy(p_hbm.at[0], dq, loads.at[1]),
         pltpu.make_async_copy(wq_hbm, wq, loads.at[2]),
         pltpu.make_async_copy(wk_hbm, wkv.at[:, :CHANNEL_DIM], loads.at[3]),
         pltpu.make_async_copy(wv_hbm, wkv.at[:, CHANNEL_DIM:], loads.at[4]),
@@ -354,10 +354,10 @@
         copy.start()
     greet([places["sibling"], places["head_up"], places["head_down"], places["head_pair"], *around])
 
-    rows = mine.shape[3]
+    rows = mine.shape[2]
     swaps = [
         remote(
-            p_hbm.at[:, :, 1 - core, c], side.at[c],
+            p_hbm.at[pl.ds(1, 2 * RING), 1 - core, c], side.at[c],
             side_send.at[c], side_receive.at[c], places["sibling"],
         )
         for c in range(CHUNKS)
@@ -390,7 +390,7 @@
     ]
 
     def join(c, r, p):
-        return mine[r, p, c].astype(jnp.float32) + side[c, r, p].astype(jnp.float32)
+        return mine[2 * r + p, c].astype(jnp.float32) + side[c, 2 * r + p].astype(jnp.float32)
 
     local[0].wait()
     for c in range(CHUNKS):
@@ -405,9 +405,12 @@
 
     @pl.loop(0, 2 * RING)
     def _(f):
+        at = pl.ds(pl.multiple_of(f * FEATURES, FEATURES), FEATURES)
+        query_grad = jnp.concatenate(
+            [dq[k].reshape(dq.shape[1] * dq.shape[2], dq.shape[3]) for k in range(2)], axis=1
+        )
         parts[f] = lax.dot_general(
-            dq[...], wq[pl.ds(pl.multiple_of(f * FEATURES, FEATURES), FEATURES), :],
-            (((1,), (1,)), ((), ())), preferred_element_type=jnp.float32,
+            query_grad, wq[at, :], (((1,), (1,)), ((), ())), preferred_element_type=jnp.float32
         )
 
     local[3].wait()
@@ -461,10 +464,10 @@
             copy.wait_send()
 
 
-def back(query_grad, pieces, w_query, w_key, value_projection):
-    tokens, lanes = query_grad.shape
-    width = w_query.shape[0]
-    rows = tokens // CHUNKS
+def back(pieces, w_query, w_key, value_projection):
+    rows = pieces.shape[3]
+    tokens = rows * CHUNKS
+    width, lanes = w_query.shape
     vmem = pl.BlockSpec(memory_space=pltpu.VMEM)
     hbm = pl.BlockSpec(memory_space=pl.ANY)
     wide = 2 * CHANNEL_DIM
@@ -473,14 +476,14 @@
     return pl.pallas_call(
         back_kernel,
         out_shape=jax.ShapeDtypeStruct((tokens, FEATURES), bf16),
-        in_specs=[hbm] * 5,
+        in_specs=[hbm] * 4,
         out_specs=vmem,
         scratch_shapes=[
-            pltpu.VMEM((tokens, lanes), bf16),
-            pltpu.VMEM((RING, 2, CHUNKS, rows, wide), bf16),
+            pltpu.VMEM((2, CHUNKS, rows, wide), bf16),
+            pltpu.VMEM((2 * RING, CHUNKS, rows, wide), bf16),
             pltpu.VMEM((width, lanes), bf16),
             pltpu.VMEM((width, wide), bf16),
-            pltpu.VMEM((CHUNKS, RING, 2, rows, wide), bf16),
+            pltpu.VMEM((CHUNKS, 2 * RING, rows, wide), bf16),
             pltpu.VMEM((CHUNKS, RING, 2, rows, wide), bf16),
             pltpu.VMEM((CHUNKS, len(OFFSETS), rows, wide), bf16),
             pltpu.VMEM((CHUNKS, rows, wide), bf16),
@@ -502,45 +505,89 @@
             dma((CHUNKS,)),
         ],
         compiler_params=pltpu.CompilerParams(
-            collective_id=1, has_side_effects=True, vmem_limit_bytes=GRANT
+            collective_id=1, has_side_effects=True, vmem_limit_bytes=54000 * 1024
         ),
         name="back",
-    )(query_grad, pieces, w_query, w_key, value_projection)
+    )(pieces, w_query, w_key, value_projection)
 
 
 def attention_kernel(
     span_ref, length_ref, q_hbm, g_hbm, kv_hbm,
-    dq_hbm, dkv_hbm,
-    kvs, qs, gs, s_buf, d_buf, acc, dqt, q_ref, g_ref, dq_ref, dkv_ref,
+    out_hbm,
+    kvs, qs, gs, s_buf, d_buf, acc, dqt, q_ref, g_ref, dq_ref, dkv_ref, blank, row_of,
     loads, stores,
 ):
     exponent = LOG2E / math.sqrt(CHANNEL_DIM)
     scale = 1.0 / math.sqrt(CHANNEL_DIM)
     spans = span_ref.shape[0]
-
+    tokens, wide = q_ref.shape[0], 2 * CHANNEL_DIM
     local = [
         pltpu.make_async_copy(q_hbm, q_ref, loads.at[0]),
         pltpu.make_async_copy(g_hbm, g_ref, loads.at[1]),
     ]
     for copy in local:
         copy.start()
+    blank[...] = jnp.zeros_like(blank)
+
+    places = []
+    for b in range(2):
+        c = span_ref[2 * lax.axis_index("ctx") + b]
+        first = 0
+        end = 0
+        for k in range(length_ref.shape[0]):
+            end = end + length_ref[k]
+            first = jnp.where(c * HALF >= end, end, first)
+        places.append((c, first // TILE, c // (TILE // HALF) + 1))
+
+    def reached(p):
+        t = p // (TILE // HALF)
+        return jnp.logical_or(
+            *[jnp.logical_and(t >= low, t < high) for c, low, high in places]
+        )
+
+    def rows_at(n):
+        return pl.ds(pl.multiple_of(n * HALF, HALF), HALF)
+
+    def block_in(r, p):
+        return pltpu.make_async_copy(
+            kv_hbm.at[rows_at(r), :], kvs.at[rows_at(p), :], loads.at[2]
+        )
+
+    def block_out(block, r):
+        return pltpu.make_async_copy(
+            block, out_hbm.at[rows_at(r + 2 * tokens // HALF), :], stores.at[1]
+        )
 
     @pl.loop(0, spans)
     def _(r):
         p = span_ref[r]
-        pltpu.make_async_copy(
-            kv_hbm.at[pl.ds(pl.multiple_of(r * HALF, HALF), HALF), :],
-            kvs.at[pl.ds(pl.multiple_of(p * HALF, HALF), HALF), :],
-            loads.at[2],
-        ).start()
+        row_of[p] = r
+
+        @pl.when(reached(p))
+        def _():
+            block_in(r, p).start()
+
+        @pl.when(jnp.logical_not(reached(p)))
+        def _():
+            block_out(blank, r).start()
+
+    for c, low, high in places:
+
+        @pl.loop(low, high)
+        def _(t):
+            acc[pl.ds(pl.multiple_of(t * TILE, TILE), TILE), :] = jnp.zeros((TILE, wide), jnp.float32)
+
+    for copy in local:
+        copy.wait()
 
     @pl.loop(0, spans)
     def _(r):
-        acc[pl.ds(pl.multiple_of(r * HALF, HALF), HALF), :] = jnp.zeros((HALF, 2 * CHANNEL_DIM), jnp.float32)
-
-    for copy in local:
-        copy.wait()
-    pltpu.make_async_copy(kv_hbm, kvs, loads.at[2]).wait()
+        p = span_ref[r]
+
+        @pl.when(reached(p))
+        def _():
+            block_in(r, p).wait()
+
     lanes = BUNDLE * HALF
     for b in range(2):
         rows = slice(b * HALF, (b + 1) * HALF)
@@ -548,17 +595,13 @@
             cols = slice(h * CHANNEL_DIM, (h + 1) * CHANNEL_DIM)
             qs[h * HALF : (h + 1) * HALF, :] = q_ref[rows, cols]
             gs[h * HALF : (h + 1) * HALF, :] = g_ref[rows, cols]
-        c = span_ref[2 * lax.axis_index("ctx") + b]
+        c, low, high = places[b]
         position = c * HALF + lax.broadcasted_iota(jnp.int32, (1, HALF), 1)
         start = jnp.zeros((1, HALF), jnp.int32)
-        first = 0
         end = 0
         for k in range(length_ref.shape[0]):
             end = end + length_ref[k]
             start = jnp.where(position >= end, end, start)
-            first = jnp.where(c * HALF >= end, end, first)
-        low = first // TILE
-        high = c // (TILE // HALF) + 1
 
         def gather_stats(t, carry):
             top, total, inner = carry
@@ -608,24 +651,38 @@
             )
 
         for h in range(BUNDLE):
-            dq_ref[rows, h * CHANNEL_DIM : (h + 1) * CHANNEL_DIM] = (
+            to = slice(h // 2 * tokens + b * HALF, h // 2 * tokens + (b + 1) * HALF)
+            dq_ref[to, h % 2 * CHANNEL_DIM : (h % 2 + 1) * CHANNEL_DIM] = (
                 (dqt[:, h * HALF : (h + 1) * HALF] * scale).T.astype(jnp.bfloat16)
             )
 
-    grads = pltpu.make_async_copy(dq_ref, dq_hbm, stores.at[0])
+    grads = pltpu.make_async_copy(dq_ref, out_hbm.at[pl.ds(0, 2 * tokens), :], stores.at[0])
     grads.start()
 
-    @pl.loop(0, spans)
-    def _(r):
-        p = span_ref[r]
-        at = pl.ds(pl.multiple_of(p * HALF, HALF), HALF)
-        to = pl.ds(pl.multiple_of(r * HALF, HALF), HALF)
+    def finish(p):
+        r = row_of[p]
+        at, to = rows_at(p), rows_at(r)
         dkv_ref[to, :CHANNEL_DIM] = (acc[at, :CHANNEL_DIM] * scale).astype(jnp.bfloat16)
         dkv_ref[to, CHANNEL_DIM:] = acc[at, CHANNEL_DIM:].astype(jnp.bfloat16)
-        pltpu.make_async_copy(dkv_ref.at[to, :], dkv_hbm.at[to, :], stores.at[1]).start()
+        block_out(dkv_ref.at[to, :], r).start()
+
+    for b, (c, low, high) in enumerate(places):
+
+        @pl.loop(low, high)
+        def _(t):
+            fresh = True
+            if b:
+                fresh = jnp.logical_or(t < places[0][1], t >= places[0][2])
+
+            @pl.when(fresh)
+            def _():
+                for k in range(TILE // HALF):
+                    finish(t * (TILE // HALF) + k)
 
     grads.wait()
-    pltpu.make_async_copy(dkv_ref, dkv_hbm, stores.at[1]).wait()
+    pltpu.make_async_copy(
+        dkv_ref, out_hbm.at[pl.ds(2 * tokens, dkv_ref.shape[0]), :], stores.at[1]
+    ).wait()
 
 
 def attention(q, g, kv, span_order, doc_lengths):
@@ -636,12 +693,9 @@
     lanes = BUNDLE * HALF
     return pl.pallas_call(
         attention_kernel,
-        out_shape=(
-            jax.ShapeDtypeStruct((tokens, lanes), jnp.bfloat16),
-            jax.ShapeDtypeStruct((length, 2 * CHANNEL_DIM), jnp.bfloat16),
-        ),
+        out_shape=jax.ShapeDtypeStruct((2 * tokens + length, 2 * CHANNEL_DIM), jnp.bfloat16),
         in_specs=[smem, smem, hbm, hbm, hbm],
-        out_specs=(hbm, hbm),
+        out_specs=hbm,
         scratch_shapes=[
             pltpu.VMEM((length, 2 * CHANNEL_DIM), jnp.bfloat16),
             pltpu.VMEM((lanes, CHANNEL_DIM), jnp.bfloat16),
@@ -652,8 +706,10 @@
             pltpu.VMEM((CHANNEL_DIM, lanes), jnp.float32),
             pltpu.VMEM((tokens, lanes), jnp.bfloat16),
             pltpu.VMEM((tokens, lanes), jnp.bfloat16),
-            pltpu.VMEM((tokens, lanes), jnp.bfloat16),
+            pltpu.VMEM((2 * tokens, 2 * CHANNEL_DIM), jnp.bfloat16),
             pltpu.VMEM((length, 2 * CHANNEL_DIM), jnp.bfloat16),
+            pltpu.VMEM((HALF, 2 * CHANNEL_DIM), jnp.bfloat16),
+            pltpu.SMEM((length // HALF,), jnp.int32),
             pltpu.SemaphoreType.DMA((3,)),
             pltpu.SemaphoreType.DMA((2,)),
         ],
@@ -668,11 +724,11 @@
     query, context_grad, gathered = front(
         inputs, out_grad, w_query, w_key, value_projection, w_out, peers
     )
-    query_grad, pieces = attention(
+    pieces = attention(
         query, context_grad, gathered.reshape(peers * tokens, -1), span_order, doc_lengths
     )
-    pieces = pieces.reshape(RING, 2, 2, CHUNKS, tokens // CHUNKS, -1)
-    return back(query_grad, pieces, w_query, w_key, value_projection)
+    pieces = pieces.reshape(1 + 2 * RING, 2, CHUNKS, tokens // CHUNKS, -1)
+    return back(pieces, w_query, w_key, value_projection)
 
 
 def solution(mesh):

time: 76.7 us -> 74.8 us (0.975)
  local copies, waits for them, and re-layouts: 1.67 us -> 0.71 us
  Pallas kernels: 74.8 us -> 73.9 us
    unnamed x1, local copies, waits for them, and re-layouts: 1.67 us -> 0.71 us
where the time goes in v2:
time: 74.8 us; the launch traced here: 74.6 us
  Pallas kernels  73.9 us (99%)
    pallas_call x1, Pallas kernels, back(): pl.pallas_call(back_kernel, out_shape=jax.ShapeDtypeStruct((tokens, FEATU...  38.2 us
    pallas_call x1, Pallas kernels, front(): pl.pallas_call(front_kernel, out_shape=(jax.ShapeDtypeStruct((tokens, lan...  28 us
    pallas_call x1, Pallas kernels, attention(): pl.pallas_call(attention_kernel, out_shape=jax.ShapeDtypeStruct((2 * toke...  7.75 us

profile of v2, /device:TPU:1, one launch (start us, length us, event | category | flops | bytes accessed | tf_op | source)
XLA Modules:
  0.0 74.6 jit_solution(10638267519799683633)
XLA Ops:
  0.0 28.0 %front.1 = (bf16[256,512]{1,0:T(8,128)(2,1)}, bf16[256,512]{1,0:T(8,128)(2,1)}, bf16[16,256,256]{2,1,0:T(8,128)(2,1)}) custom-call(bf16[256,4096]{1,0:T(8,128)(2,1)} %x_hbm.1, bf16[256,512]{1,0:T(8,128)(2,1)} %og_hbm.1, bf16[4096,512]{1,0:T(8,128)(2,1)} %wq_hbm.3, bf16[4096,128]{1,0:T(8,128)(2,1)} %wk_hbm.3, bf16[4096,128]{1,0:T(8,128)(2,1)} %wv_hbm.3, ...), custom_call_target="tpu_custom_call" | custom-call | tf_op jit(solution)/shard_map/front/pallas_call | solution.py:251
  28.0 7.8 %attention.1 = bf16[4608,256]{1,0:T(8,128)(2,1)} custom-call(s32[32]{0:T(128)} %span_ref.1, s32[8]{0:T(128)} %length_ref.1, bf16[256,512]{1,0:T(8,128)(2,1)} %get-tuple-element.8.q_hbm, bf16[256,512]{1,0:T(8,128)(2,1)} %get-tuple-element.9.g_hbm, bf16[4096,256]{1,0:T(8,128)(2,1)} %bitcast.3), custom_call_target="tpu_custom_call" | custom-call | tf_op jit(solution)/shard_map/attention/pallas_call | solution.py:694
  35.7 38.2 %back.1 = bf16[256,512]{1,0:T(8,128)(2,1)S(1)} custom-call(bf16[9,2,4,64,256]{4,3,2,1,0:T(8,128)(2,1)} %bitcast.2, bf16[4096,512]{1,0:T(8,128)(2,1)} %wq_hbm.3, bf16[4096,128]{1,0:T(8,128)(2,1)} %wk_hbm.3, bf16[4096,128]{1,0:T(8,128)(2,1)} %wv_hbm.3), custom_call_target="tpu_custom_call" | custom-call | tf_op jit(solution)/shard_map/back/pallas_call | solution.py:476
  73.9 0.7 copy.10

commit v3 on v2

--- a/solution.py
+++ b/solution.py
@@ -15,7 +15,7 @@
 TILE = 256
 RING = 4
 FEATURES = 512
-CHUNKS = 4
+PARTS = tuple(pl.ds(*cut) for cut in ((0, 64), (64, 64), (128, 64), (192, 64)))
 OFFSETS = ((2, 1), (2, 0), (1, 1), (3, 1), (1, 0), (3, 0), (0, 1))
 LOG2E = 1.4426950408889634
 MASKED = -1e30
@@ -62,11 +62,18 @@
 
 
 class Gather:
-    def __init__(self, source, block, half, pair, ring, sends, receives, up, down, across):
+    def __init__(self, source, block, pair, ring, sends, receives, up, down, across):
         other = 1 - pair
         before, after, opposite = (ring + 3) % RING, (ring + 1) % RING, (ring + 2) % RING
         self.copies = []
         own = block(pair, ring)
+
+        def half(p, r, k, start=0, size=HALF):
+            return block(p, r).at[pl.ds(k * HALF + start, size), :]
+
+        def quarter(p, r, k, q):
+            return half(p, r, k, q * HALF // 2, HALF // 2)
+
         plan = [
             (source(0), half(pair, ring, 0), half(pair, before, 0), up),
             (source(1), half(pair, ring, 1), half(pair, after, 1), down),
@@ -79,8 +86,22 @@
             (half(other, ring, 1), half(other, ring, 1), half(other, after, 1), down),
             (half(other, ring, 1), half(other, ring, 1), half(other, before, 1), up),
             (half(other, ring, 0), half(other, ring, 0), half(other, after, 0), down),
-            (half(other, before, 0), half(other, before, 0), half(other, opposite, 0), up),
-            (half(other, after, 1), half(other, after, 1), half(other, opposite, 1), down),
+            (
+                quarter(other, before, 0, 0), quarter(other, before, 0, 0),
+                quarter(other, opposite, 0, 0), up,
+            ),
+            (
+                quarter(other, after, 1, 0), quarter(other, after, 1, 0),
+                quarter(other, opposite, 1, 0), down,
+            ),
+            (
+                quarter(pair, opposite, 0, 1), quarter(pair, opposite, 0, 1),
+                quarter(other, opposite, 0, 1), across,
+            ),
+            (
+                quarter(pair, opposite, 1, 1), quarter(pair, opposite, 1, 1),
+                quarter(other, opposite, 1, 1), across,
+            ),
         ]
         for k, (src, dst, landed, place) in enumerate(plan):
             self.copies.append(
@@ -119,7 +140,7 @@
         pltpu.make_async_copy(og_hbm, og.at[me], loads.at[4]),
         pltpu.make_async_copy(wo_hbm, wo, loads.at[5]),
     ]
-    for copy in local:
+    for copy in local[:3]:
         copy.start()
     saved = [
         pltpu.make_async_copy(q_ref, q_hbm, stores.at[0]),
@@ -131,11 +152,12 @@
     heads = Gather(
         lambda k: og_hbm if k is None else og_hbm.at[pl.ds(k * HALF, HALF), :],
         lambda p, r: og.at[p * RING + r],
-        lambda p, r, k: og.at[p * RING + r, pl.ds(k * HALF, HALF), :],
         far, depth, head_send, head_receive,
         places["head_up"], places["head_down"], places["head_pair"],
     )
     heads.start(0, 1, 2, 3, 4)
+    for copy in local[3:]:
+        copy.start()
 
     def slot(p, r, c=core):
         return r * 4 + p * 2 + c
@@ -145,7 +167,6 @@
         if k is None
         else kv_ref.at[slot(near, line), pl.ds(k * HALF, HALF), :],
         lambda p, r: kv_ref.at[slot(p, r)],
-        lambda p, r, k: kv_ref.at[slot(p, r), pl.ds(k * HALF, HALF), :],
         near, line, ctx_send, ctx_receive,
         places["ctx_up"], places["ctx_down"], places["ctx_pair"],
     )
@@ -176,11 +197,26 @@
     kv_ref[slot(near, line)] = jnp.dot(
         x[...], wkv[...], preferred_element_type=jnp.float32
     ).astype(jnp.bfloat16)
+    def query(k):
+        columns = slice(k * wq.shape[1] // 2, (k + 1) * wq.shape[1] // 2)
+        q_ref[:, columns] = jnp.dot(
+            x[...], wq[:, columns], preferred_element_type=jnp.float32
+        ).astype(jnp.bfloat16)
+
+    def keep(at):
+        pltpu.make_async_copy(kv_ref.at[at], kv_hbm.at[at], stores.at[1]).start()
+
+    def share(k):
+        passed[k][0].start()
+        keep(slot(*turns[k]))
+
     local[3].wait()
-    q_ref[...] = jnp.dot(x[...], wq[...], preferred_element_type=jnp.float32).astype(jnp.bfloat16)
+    query(0)
     spread.start(0, 1, 2, 3, 4)
-    passed[0][0].start()
+    share(0)
+    query(1)
     saved[0].start()
+    before, after, opposite = (depth + 3) % RING, (depth + 1) % RING, (depth + 2) % RING
     heads.arrive(0)
     heads.start(5)
     heads.arrive(1)
@@ -188,52 +224,56 @@
     local[4].wait()
     local[5].wait()
     acc[...] = features(far, depth)
-
-    before, after, opposite = (depth + 3) % RING, (depth + 1) % RING, (depth + 2) % RING
-    spread.arrive(2)
-    spread.start(7, 8, 9, 10)
-    passed[4][0].start()
     spread.arrive(0)
     spread.start(5)
     spread.arrive(1)
     spread.start(6)
-    heads.arrive(2)
-    heads.start(7, 8, 9, 10)
     heads.arrive(3)
     acc[...] += features(far, before)
+    spread.arrive(2)
+    spread.start(7, 8, 9, 10)
+    share(4)
     heads.arrive(4)
     acc[...] += features(far, after)
     spread.arrive(3)
-    passed[1][0].start()
+    share(1)
     spread.arrive(4)
-    passed[2][0].start()
+    share(2)
+    heads.arrive(2)
+    heads.start(7, 8, 9, 10)
+    acc[...] += features(1 - far, depth)
+    spread.arrive(5)
+    spread.start(13)
+    spread.arrive(6)
+    spread.start(14)
+    share(3)
+    heads.arrive(5)
+    heads.start(13)
+    heads.arrive(6)
+    heads.start(14)
+    acc[...] += features(far, opposite)
     spread.arrive(7)
     spread.start(11)
     spread.arrive(8)
     spread.start(12)
-    acc[...] += features(1 - far, depth)
-    heads.arrive(5, 6)
-    acc[...] += features(far, opposite)
-    spread.arrive(5, 6)
-    passed[3][0].start()
     spread.arrive(9)
-    passed[5][0].start()
+    share(5)
     spread.arrive(10)
-    passed[6][0].start()
+    share(6)
     heads.arrive(7)
     heads.start(11)
     heads.arrive(8)
     heads.start(12)
-    spread.arrive(11, 12)
-    passed[7][0].start()
+    spread.arrive(11, 12, 13, 14)
+    share(7)
     heads.arrive(9)
     acc[...] += features(1 - far, before)
     heads.arrive(10)
     acc[...] += features(1 - far, after)
-    for sent, landed in passed:
+    for k, (sent, landed) in enumerate(passed):
         landed.wait_recv()
-    saved[1].start()
-    heads.arrive(11, 12)
+        keep(slot(*turns[k], 1 - core))
+    heads.arrive(11, 12, 13, 14)
     g_ref[...] = (acc[...] + features(1 - far, opposite)).astype(jnp.bfloat16)
     saved[2].start()
     heads.drain()
@@ -269,10 +309,10 @@
             pltpu.VMEM((peers, tokens, 2 * CHANNEL_DIM), jnp.bfloat16),
             pltpu.SemaphoreType.DMA((6,)),
             pltpu.SemaphoreType.DMA((3,)),
-            pltpu.SemaphoreType.DMA((13,)),
-            pltpu.SemaphoreType.DMA((13,)),
-            pltpu.SemaphoreType.DMA((13,)),
-            pltpu.SemaphoreType.DMA((13,)),
+            pltpu.SemaphoreType.DMA((15,)),
+            pltpu.SemaphoreType.DMA((15,)),
+            pltpu.SemaphoreType.DMA((15,)),
+            pltpu.SemaphoreType.DMA((15,)),
             pltpu.SemaphoreType.DMA((8,)),
             pltpu.SemaphoreType.DMA((8,)),
         ],
@@ -354,109 +394,120 @@
         copy.start()
     greet([places["sibling"], places["head_up"], places["head_down"], places["head_pair"], *around])
 
-    rows = mine.shape[2]
     swaps = [
         remote(
-            p_hbm.at[pl.ds(1, 2 * RING), 1 - core, c], side.at[c],
+            p_hbm.at[pl.ds(1, 2 * RING), 1 - core, rows], side.at[:, rows],
             side_send.at[c], side_receive.at[c], places["sibling"],
         )
-        for c in range(CHUNKS)
-    ]
-    for copy in swaps:
-        copy.start()
+        for c, rows in enumerate(PARTS)
+    ]
+    swaps[0].start()
     sends = [
         [
             remote(
-                held.at[c, r, p], inbox.at[c, k],
+                held.at[r, p, rows], inbox.at[k, rows],
                 ctx_send.at[c, k], ctx_receive.at[c, k], around[k],
             )
             for k, (r, p) in enumerate(others)
         ]
-        for c in range(CHUNKS)
+        for c, rows in enumerate(PARTS)
     ]
     rounds = [
         Reduce(
-            leaving.at[c], gone.at[c], sums.at[c], depth,
-            head_send.at[c], head_receive.at[c], places["head_up"], places["head_down"],
-        )
-        for c in range(CHUNKS)
+            leaving.at[:, :, rows],
+            gone.at[:, :, pl.ds(rows.start // 2, rows.size // 2)],
+            sums.at[:, :, rows],
+            depth, head_send.at[c], head_receive.at[c], places["head_up"], places["head_down"],
+        )
+        for c, rows in enumerate(PARTS)
     ]
     across = [
         remote(
-            crossing.at[c], crossed.at[c],
+            crossing.at[rows], crossed.at[rows],
             pair_send.at[c], pair_receive.at[c], places["head_pair"],
         )
-        for c in range(CHUNKS)
-    ]
-
-    def join(c, r, p):
-        return mine[2 * r + p, c].astype(jnp.float32) + side[c, 2 * r + p].astype(jnp.float32)
-
-    local[0].wait()
-    for c in range(CHUNKS):
+        for c, rows in enumerate(PARTS)
+    ]
+
+    def join(rows, r, p):
+        return mine[2 * r + p, rows].astype(jnp.float32) + side[2 * r + p, rows].astype(jnp.float32)
+
+    def pass_on(c):
+        rows = PARTS[c]
         swaps[c].wait_recv()
+        if c + 1 < len(PARTS):
+            swaps[c + 1].start()
         for k, (r, p) in enumerate(others):
-            held[c, r, p] = join(c, r, p).astype(jnp.bfloat16)
+            held[r, p, rows] = join(rows, r, p).astype(jnp.bfloat16)
         for copy in sends[c]:
             copy.start()
 
-    local[1].wait()
-    local[2].wait()
-
-    @pl.loop(0, 2 * RING)
-    def _(f):
-        at = pl.ds(pl.multiple_of(f * FEATURES, FEATURES), FEATURES)
-        query_grad = jnp.concatenate(
-            [dq[k].reshape(dq.shape[1] * dq.shape[2], dq.shape[3]) for k in range(2)], axis=1
-        )
-        parts[f] = lax.dot_general(
-            query_grad, wq[at, :], (((1,), (1,)), ((), ())), preferred_element_type=jnp.float32
-        )
-
-    local[3].wait()
-    local[4].wait()
-
-    def term(c, f):
-        return parts[f, c * rows : (c + 1) * rows, :] + lax.dot_general(
-            dkv[c], wkv[pl.ds(pl.multiple_of(f * FEATURES, FEATURES), FEATURES), :],
+    def query_parts(low, high):
+        @pl.loop(low, high)
+        def _(f):
+            at = pl.ds(pl.multiple_of(f * FEATURES, FEATURES), FEATURES)
+            query_grad = jnp.concatenate([dq[0], dq[1]], axis=1)
+            parts[f] = lax.dot_general(
+                query_grad, wq[at, :], (((1,), (1,)), ((), ())),
+                preferred_element_type=jnp.float32,
+            )
+
+    def term(rows, f):
+        return parts[f, rows, :] + lax.dot_general(
+            dkv[rows], wkv[pl.ds(pl.multiple_of(f * FEATURES, FEATURES), FEATURES), :],
             (((1,), (1,)), ((), ())), preferred_element_type=jnp.float32,
         )
 
     def issue(c):
-        total = join(c, line, near)
+        rows = PARTS[c]
+        total = join(rows, line, near)
         for k in range(len(sends[c])):
             sends[c][k].wait_recv()
-            total = total + inbox[c, k].astype(jnp.float32)
-        dkv[c] = total.astype(jnp.bfloat16)
+            total = total + inbox[k, rows].astype(jnp.float32)
+        dkv[rows] = total.astype(jnp.bfloat16)
         for d, ready in ((2, (0, 1)), (1, (2,)), (3, (3,))):
             r = (depth + d) % RING
             for p in range(2):
-                leaving[c, r, p] = term(c, p * RING + r).astype(jnp.bfloat16)
+                leaving[r, p, rows] = term(rows, p * RING + r).astype(jnp.bfloat16)
             rounds[c].start(*ready)
         for p in range(2):
-            left[c, p] = term(c, p * RING + depth)
+            left[p, rows] = term(rows, p * RING + depth)
 
     def cross(c):
+        rows = PARTS[c]
         rounds[c].arrive()
-        crossing[c] = (left[c, 1 - far] + rounds[c].total(1 - far)).astype(jnp.bfloat16)
+        crossing[rows] = (left[1 - far, rows] + rounds[c].total(1 - far)).astype(jnp.bfloat16)
         across[c].start()
-        left[c, far] = left[c, far] + rounds[c].total(far)
-
+        left[far, rows] = left[far, rows] + rounds[c].total(far)
+
+    last = len(PARTS) - 1
+    local[0].wait()
+    pass_on(0)
+    local[1].wait()
+    local[2].wait()
+    query_parts(0, RING)
+    pass_on(1)
+    query_parts(RING, 2 * RING)
+    pass_on(2)
+    local[3].wait()
+    local[4].wait()
     issue(0)
-    for c in range(1, CHUNKS):
+    for c in range(3, len(PARTS)):
+        pass_on(c)
+    for c in range(1, len(PARTS)):
         issue(c)
         rounds[c - 1].relay()
         if c > 1:
             cross(c - 2)
-    rounds[CHUNKS - 1].relay()
-    cross(CHUNKS - 2)
-    cross(CHUNKS - 1)
-    for c in range(CHUNKS):
+    rounds[last].relay()
+    cross(last - 1)
+    cross(last)
+    for c, rows in enumerate(PARTS):
         across[c].wait_recv()
-        out_ref[c * rows : (c + 1) * rows, :] = (
-            left[c, far] + crossed[c].astype(jnp.float32)
+        out_ref[rows, :] = (
+            left[far, rows] + crossed[rows].astype(jnp.float32)
         ).astype(jnp.bfloat16)
-    for c in range(CHUNKS):
+    for c in range(len(PARTS)):
         swaps[c].wait_send()
         across[c].wait_send()
         rounds[c].drain()
@@ -465,8 +516,8 @@
 
 
 def back(pieces, w_query, w_key, value_projection):
-    rows = pieces.shape[3]
-    tokens = rows * CHUNKS
+    tokens = pieces.shape[2]
+    chunks = len(PARTS)
     width, lanes = w_query.shape
     vmem = pl.BlockSpec(memory_space=pltpu.VMEM)
     hbm = pl.BlockSpec(memory_space=pl.ANY)
@@ -479,30 +530,30 @@
         in_specs=[hbm] * 4,
         out_specs=vmem,
         scratch_shapes=[
-            pltpu.VMEM((2, CHUNKS, rows, wide), bf16),
-            pltpu.VMEM((2 * RING, CHUNKS, rows, wide), bf16),
+            pltpu.VMEM((2, tokens, wide), bf16),
+            pltpu.VMEM((2 * RING, tokens, wide), bf16),
             pltpu.VMEM((width, lanes), bf16),
             pltpu.VMEM((width, wide), bf16),
-            pltpu.VMEM((CHUNKS, 2 * RING, rows, wide), bf16),
-            pltpu.VMEM((CHUNKS, RING, 2, rows, wide), bf16),
-            pltpu.VMEM((CHUNKS, len(OFFSETS), rows, wide), bf16),
-            pltpu.VMEM((CHUNKS, rows, wide), bf16),
+            pltpu.VMEM((2 * RING, tokens, wide), bf16),
+            pltpu.VMEM((RING, 2, tokens, wide), bf16),
+            pltpu.VMEM((len(OFFSETS), tokens, wide), bf16),
+            pltpu.VMEM((tokens, wide), bf16),
             pltpu.VMEM((2 * RING, tokens, FEATURES), f32),
-            pltpu.VMEM((CHUNKS, RING, 2, rows, FEATURES), bf16),
-            pltpu.VMEM((CHUNKS, 2, rows, FEATURES), f32),
-            pltpu.VMEM((CHUNKS, 2, 2, rows // 2, FEATURES), bf16),
-            pltpu.VMEM((CHUNKS, 2, 2, rows, FEATURES), bf16),
-            pltpu.VMEM((CHUNKS, rows, FEATURES), bf16),
-            pltpu.VMEM((CHUNKS, rows, FEATURES), bf16),
+            pltpu.VMEM((RING, 2, tokens, FEATURES), bf16),
+            pltpu.VMEM((2, tokens, FEATURES), f32),
+            pltpu.VMEM((2, 2, tokens // 2, FEATURES), bf16),
+            pltpu.VMEM((2, 2, tokens, FEATURES), bf16),
+            pltpu.VMEM((tokens, FEATURES), bf16),
+            pltpu.VMEM((tokens, FEATURES), bf16),
             dma((5,)),
-            dma((CHUNKS,)),
-            dma((CHUNKS,)),
-            dma((CHUNKS, len(OFFSETS))),
-            dma((CHUNKS, len(OFFSETS))),
-            dma((CHUNKS, 6)),
-            dma((CHUNKS, 6)),
-            dma((CHUNKS,)),
-            dma((CHUNKS,)),
+            dma((chunks,)),
+            dma((chunks,)),
+            dma((chunks, len(OFFSETS))),
+            dma((chunks, len(OFFSETS))),
+            dma((chunks, 6)),
+            dma((chunks, 6)),
+            dma((chunks,)),
+            dma((chunks,)),
         ],
         compiler_params=pltpu.CompilerParams(
             collective_id=1, has_side_effects=True, vmem_limit_bytes=54000 * 1024
@@ -630,15 +681,26 @@
             return fresh, total, inner
 
         zero = jnp.zeros((1, lanes), jnp.float32)
+        pairs = (high - low) // 2
+        odd = low + 2 * pairs
         top, total, inner = lax.fori_loop(
-            low, high, gather_stats, (jnp.full((1, lanes), MASKED, jnp.float32), zero, zero)
+            odd,
+            high,
+            gather_stats,
+            lax.fori_loop(
+                0,
+                pairs,
+                lambda k, carry: gather_stats(
+                    low + 2 * k + 1, gather_stats(low + 2 * k, carry)
+                ),
+                (jnp.full((1, lanes), MASKED, jnp.float32), zero, zero),
+            ),
         )
         delta = inner / total
         level = top + jnp.log2(total)
         dqt[...] = jnp.zeros_like(dqt)
 
-        @pl.loop(low, high)
-        def _(t):
+        def spread_grads(t):
             at = pl.ds(pl.multiple_of(t * TILE, TILE), TILE)
             probability = jnp.exp2(s_buf[at, :] - level)
             score_grad = (probability * (d_buf[at, :] - delta)).astype(jnp.bfloat16)
@@ -649,6 +711,15 @@
                 kvs[at, :CHANNEL_DIM], score_grad, (((0,), (0,)), ((), ())),
                 preferred_element_type=jnp.float32,
             )
+
+        @pl.loop(0, pairs)
+        def _(k):
+            spread_grads(low + 2 * k)
+            spread_grads(low + 2 * k + 1)
+
+        @pl.loop(odd, high)
+        def _(t):
+            spread_grads(t)
 
         for h in range(BUNDLE):
             to = slice(h // 2 * tokens + b * HALF, h // 2 * tokens + (b + 1) * HALF)
@@ -727,7 +798,7 @@
     pieces = attention(
         query, context_grad, gathered.reshape(peers * tokens, -1), span_order, doc_lengths
     )
-    pieces = pieces.reshape(1 + 2 * RING, 2, CHUNKS, tokens // CHUNKS, -1)
+    pieces = pieces.reshape(1 + 2 * RING, 2, tokens, -1)
     return back(pieces, w_query, w_key, value_projection)
 
 

time: 74.8 us -> 72.1 us (0.964)
  Pallas kernels: 73.9 us -> 71 us
    pallas_call x1, Pallas kernels: 38.2 us -> 36.7 us  [back(): pl.pallas_call(back_kernel, out_shape=jax.ShapeDtypeStruct((tokens, FEATU...]
where the time goes in v3:
time: 72.1 us; the launch traced here: 71.8 us
  Pallas kernels  71 us (98%)
    pallas_call x1, Pallas kernels, back(): pl.pallas_call(back_kernel, out_shape=jax.ShapeDtypeStruct((tokens, FEATU...  36.7 us
    pallas_call x1, Pallas kernels, front(): pl.pallas_call(front_kernel, out_shape=(jax.ShapeDtypeStruct((tokens, lan...  27.3 us
    pallas_call x1, Pallas kernels, attention(): pl.pallas_call(attention_kernel, out_shape=jax.ShapeDtypeStruct((2 * toke...  7.11 us

profile of v3, /device:TPU:1, one launch (start us, length us, event | category | flops | bytes accessed | tf_op | source)
XLA Modules:
  0.0 71.8 jit_solution(689254660502672881)
XLA Ops:
  0.0 27.3 %front.1 = (bf16[256,512]{1,0:T(8,128)(2,1)}, bf16[256,512]{1,0:T(8,128)(2,1)}, bf16[16,256,256]{2,1,0:T(8,128)(2,1)}) custom-call(bf16[256,4096]{1,0:T(8,128)(2,1)} %x_hbm.1, bf16[256,512]{1,0:T(8,128)(2,1)} %og_hbm.1, bf16[4096,512]{1,0:T(8,128)(2,1)} %wq_hbm.3, bf16[4096,128]{1,0:T(8,128)(2,1)} %wk_hbm.3, bf16[4096,128]{1,0:T(8,128)(2,1)} %wv_hbm.3, ...), custom_call_target="tpu_custom_call" | custom-call | tf_op jit(solution)/shard_map/front/pallas_call | solution.py:291
  27.3 7.1 %attention.1 = bf16[4608,256]{1,0:T(8,128)(2,1)} custom-call(s32[32]{0:T(128)} %span_ref.1, s32[8]{0:T(128)} %length_ref.1, bf16[256,512]{1,0:T(8,128)(2,1)} %get-tuple-element.8.q_hbm, bf16[256,512]{1,0:T(8,128)(2,1)} %get-tuple-element.9.g_hbm, bf16[4096,256]{1,0:T(8,128)(2,1)} %bitcast.3), custom_call_target="tpu_custom_call" | custom-call | tf_op jit(solution)/shard_map/attention/pallas_call | solution.py:765
  34.4 36.7 %back.1 = bf16[256,512]{1,0:T(8,128)(2,1)S(1)} custom-call(bf16[9,2,256,256]{3,2,1,0:T(8,128)(2,1)} %bitcast.2, bf16[4096,512]{1,0:T(8,128)(2,1)} %wq_hbm.3, bf16[4096,128]{1,0:T(8,128)(2,1)} %wk_hbm.3, bf16[4096,128]{1,0:T(8,128)(2,1)} %wv_hbm.3), custom_call_target="tpu_custom_call" | custom-call | tf_op jit(solution)/shard_map/back/pallas_call | solution.py:527
  71.1 0.7 copy.10

commit v4 on v3

--- a/solution.py
+++ b/solution.py
@@ -19,6 +19,7 @@
 OFFSETS = ((2, 1), (2, 0), (1, 1), (3, 1), (1, 0), (3, 0), (0, 1))
 LOG2E = 1.4426950408889634
 MASKED = -1e30
+OWN = ("u0", "d1", "x0", "x2", "u1", "d0", "x1", "x3")
 GRANT = 60 * 1024 * 1024
 MESH = pl.DeviceIdType.MESH
 
@@ -56,71 +57,72 @@
         "ctx_up": (head, ctx_of((line + 1) % RING, near, core)),
         "ctx_down": (head, ctx_of((line + 3) % RING, near, core)),
         "ctx_pair": (head, ctx_of(line, 1 - near, core)),
+        "ctx_far": (head, ctx_of((line + 2) % RING, near, core)),
         "sibling": (head, ctx_of(line, near, 1 - core)),
     }
     return places, (far, depth), (line, near, core)
 
 
 class Gather:
-    def __init__(self, source, block, pair, ring, sends, receives, up, down, across):
+    def __init__(self, source, block, pair, ring, sends, receives, up, down, across, opposed=None):
         other = 1 - pair
         before, after, opposite = (ring + 3) % RING, (ring + 1) % RING, (ring + 2) % RING
-        self.copies = []
-        own = block(pair, ring)
-
-        def half(p, r, k, start=0, size=HALF):
-            return block(p, r).at[pl.ds(k * HALF + start, size), :]
-
-        def quarter(p, r, k, q):
-            return half(p, r, k, q * HALF // 2, HALF // 2)
-
-        plan = [
-            (source(0), half(pair, ring, 0), half(pair, before, 0), up),
-            (source(1), half(pair, ring, 1), half(pair, after, 1), down),
-            (source(None), own, block(other, ring), across),
-            (source(1), half(pair, ring, 1), half(pair, before, 1), up),
-            (source(0), half(pair, ring, 0), half(pair, after, 0), down),
-            (half(pair, before, 0), half(pair, before, 0), half(pair, opposite, 0), up),
-            (half(pair, after, 1), half(pair, after, 1), half(pair, opposite, 1), down),
-            (half(other, ring, 0), half(other, ring, 0), half(other, before, 0), up),
-            (half(other, ring, 1), half(other, ring, 1), half(other, after, 1), down),
-            (half(other, ring, 1), half(other, ring, 1), half(other, before, 1), up),
-            (half(other, ring, 0), half(other, ring, 0), half(other, after, 0), down),
-            (
-                quarter(other, before, 0, 0), quarter(other, before, 0, 0),
-                quarter(other, opposite, 0, 0), up,
-            ),
-            (
-                quarter(other, after, 1, 0), quarter(other, after, 1, 0),
-                quarter(other, opposite, 1, 0), down,
-            ),
-            (
-                quarter(pair, opposite, 0, 1), quarter(pair, opposite, 0, 1),
-                quarter(other, opposite, 0, 1), across,
-            ),
-            (
-                quarter(pair, opposite, 1, 1), quarter(pair, opposite, 1, 1),
-                quarter(other, opposite, 1, 1), across,
-            ),
-        ]
-        for k, (src, dst, landed, place) in enumerate(plan):
-            self.copies.append(
-                (
-                    remote(src, dst, sends.at[k], receives.at[k], place),
-                    remote(landed, landed, sends.at[k], receives.at[k], place),
-                )
+        cut = HALF // 2
+
+        def part(p, r, start, size):
+            return block(p, r).at[pl.ds(start * cut, size * cut), :]
+
+        own, facing = (pair, ring), (other, ring)
+        plan = {
+            "u0": (own, (pair, before), 0, 2, up),
+            "d1": (own, (pair, after), 2, 2, down),
+            "x0": (own, facing, 0, 1, across),
+            "x2": (own, facing, 2, 1, across),
+            "u1": (own, (pair, before), 2, 2, up),
+            "d0": (own, (pair, after), 0, 2, down),
+            "x1": (own, facing, 1, 1, across),
+            "x3": (own, facing, 3, 1, across),
+            "ru": ((pair, before), (pair, opposite), 0, 2, up),
+            "rd": ((pair, after), (pair, opposite), 2, 2, down),
+            "ou0": (facing, (other, before), 0, 1, up),
+            "od2": (facing, (other, after), 2, 1, down),
+            "ou1": (facing, (other, before), 1, 2, up),
+            "od0": (facing, (other, after), 0, 1, down),
+            "od3": (facing, (other, after), 3, 1, down),
+            "xb": ((pair, before), (other, before), 3, 1, across),
+            "xa": ((pair, after), (other, after), 1, 1, across),
+            "rou": ((other, before), (other, opposite), 0, 1, up),
+            "rod": ((other, after), (other, opposite), 2, 1, down),
+            "xo1": ((pair, opposite), (other, opposite), 1, 1, across),
+            "xo3": ((pair, opposite), (other, opposite), 3, 1, across),
+        }
+        if opposed is not None:
+            plan["ou0"] = (facing, (other, before), 0, 2, up)
+            plan["ou1"] = (facing, (other, before), 2, 2, up)
+            plan["od0"] = (facing, (other, after), 0, 2, down)
+            plan["od2"] = (facing, (other, after), 2, 2, down)
+            plan["oo"] = (facing, (other, opposite), 0, 4, opposed)
+            for name in ("od3", "xb", "xa", "xo1", "xo3", "rou", "rod"):
+                del plan[name]
+        self.copies = {}
+        for k, (name, (at, to, start, size, place)) in enumerate(plan.items()):
+            there, here = part(*at, start, size), part(*to, start, size)
+            first = source(pl.ds(start * cut, size * cut)) if at is own else there
+            self.copies[name] = (
+                remote(first, there, sends.at[k], receives.at[k], place),
+                remote(here, here, sends.at[k], receives.at[k], place),
             )
 
-    def start(self, *which):
-        for k in which:
-            self.copies[k][0].start()
-
-    def arrive(self, *which):
-        for k in which:
-            self.copies[k][1].wait_recv()
+    def start(self, *names):
+        for name in names:
+            self.copies[name][0].start()
+
+    def arrive(self, *names):
+        for name in names:
+            self.copies[name][1].wait_recv()
 
     def drain(self):
-        for sent, landed in self.copies:
+        for sent, landed in self.copies.values():
             sent.wait_send()
 
 
@@ -150,12 +152,12 @@
     greet(list(places.values()))
 
     heads = Gather(
-        lambda k: og_hbm if k is None else og_hbm.at[pl.ds(k * HALF, HALF), :],
+        lambda rows: og_hbm.at[rows, :],
         lambda p, r: og.at[p * RING + r],
         far, depth, head_send, head_receive,
         places["head_up"], places["head_down"], places["head_pair"],
     )
-    heads.start(0, 1, 2, 3, 4)
+    heads.start(*OWN)
     for copy in local[3:]:
         copy.start()
 
@@ -163,12 +165,11 @@
         return r * 4 + p * 2 + c
 
     spread = Gather(
-        lambda k: kv_ref.at[slot(near, line)]
-        if k is None
-        else kv_ref.at[slot(near, line), pl.ds(k * HALF, HALF), :],
+        lambda rows: kv_ref.at[slot(near, line), rows, :],
         lambda p, r: kv_ref.at[slot(p, r)],
         near, line, ctx_send, ctx_receive,
         places["ctx_up"], places["ctx_down"], places["ctx_pair"],
+        places["ctx_far"],
     )
     turns = [(p, (line + d) % RING) for p in (near, 1 - near) for d in (0, 3, 1, 2)]
     passed = [
@@ -212,68 +213,69 @@
 
     local[3].wait()
     query(0)
-    spread.start(0, 1, 2, 3, 4)
+    spread.start(*OWN)
     share(0)
     query(1)
     saved[0].start()
     before, after, opposite = (depth + 3) % RING, (depth + 1) % RING, (depth + 2) % RING
-    heads.arrive(0)
-    heads.start(5)
-    heads.arrive(1)
-    heads.start(6)
+    heads.arrive("u0")
+    heads.start("ru")
+    heads.arrive("d1")
+    heads.start("rd")
+    heads.arrive("x0", "x2")
+    heads.start("ou0", "od2", "od0")
     local[4].wait()
     local[5].wait()
     acc[...] = features(far, depth)
-    spread.arrive(0)
-    spread.start(5)
-    spread.arrive(1)
-    spread.start(6)
-    heads.arrive(3)
+    spread.arrive("u0")
+    spread.start("ru")
+    spread.arrive("d1")
+    spread.start("rd")
+    heads.arrive("u1")
+    heads.start("xb")
+    heads.arrive("d0")
+    heads.start("xa")
+    spread.arrive("x0", "x1")
+    spread.start("ou0", "od0")
+    spread.arrive("x2", "x3")
+    spread.start("oo", "od2", "ou1")
+    share(4)
     acc[...] += features(far, before)
-    spread.arrive(2)
-    spread.start(7, 8, 9, 10)
-    share(4)
-    heads.arrive(4)
+    heads.arrive("x1")
+    heads.start("ou1")
+    heads.arrive("x3")
+    heads.start("od3")
+    spread.arrive("u1")
+    share(1)
+    spread.arrive("d0")
+    share(2)
     acc[...] += features(far, after)
-    spread.arrive(3)
-    share(1)
-    spread.arrive(4)
-    share(2)
-    heads.arrive(2)
-    heads.start(7, 8, 9, 10)
+    heads.arrive("ru")
+    heads.start("xo1")
+    heads.arrive("rd")
+    heads.start("xo3")
     acc[...] += features(1 - far, depth)
-    spread.arrive(5)
-    spread.start(13)
-    spread.arrive(6)
-    spread.start(14)
+    spread.arrive("ru", "rd")
     share(3)
-    heads.arrive(5)
-    heads.start(13)
-    heads.arrive(6)
-    heads.start(14)
+    heads.arrive("ou0")
+    heads.start("rou")
+    heads.arrive("od2")
+    heads.start("rod")
+    spread.arrive("oo")
+    share(7)
     acc[...] += features(far, opposite)
-    spread.arrive(7)
-    spread.start(11)
-    spread.arrive(8)
-    spread.start(12)
-    spread.arrive(9)
+    spread.arrive("ou0", "ou1")
     share(5)
-    spread.arrive(10)
+    spread.arrive("od0", "od2")
     share(6)
-    heads.arrive(7)
-    heads.start(11)
-    heads.arrive(8)
-    heads.start(12)
-    spread.arrive(11, 12, 13, 14)
-    share(7)
-    heads.arrive(9)
+    heads.arrive("ou1", "xb")
     acc[...] += features(1 - far, before)
-    heads.arrive(10)
+    heads.arrive("od0", "od3", "xa")
     acc[...] += features(1 - far, after)
     for k, (sent, landed) in enumerate(passed):
         landed.wait_recv()
         keep(slot(*turns[k], 1 - core))
-    heads.arrive(11, 12, 13, 14)
+    heads.arrive("rou", "rod", "xo1", "xo3")
     g_ref[...] = (acc[...] + features(1 - far, opposite)).astype(jnp.bfloat16)
     saved[2].start()
     heads.drain()
@@ -309,10 +311,10 @@
             pltpu.VMEM((peers, tokens, 2 * CHANNEL_DIM), jnp.bfloat16),
             pltpu.SemaphoreType.DMA((6,)),
             pltpu.SemaphoreType.DMA((3,)),
-            pltpu.SemaphoreType.DMA((15,)),
-            pltpu.SemaphoreType.DMA((15,)),
-            pltpu.SemaphoreType.DMA((15,)),
-            pltpu.SemaphoreType.DMA((15,)),
+            pltpu.SemaphoreType.DMA((21,)),
+            pltpu.SemaphoreType.DMA((21,)),
+            pltpu.SemaphoreType.DMA((21,)),
+            pltpu.SemaphoreType.DMA((21,)),
             pltpu.SemaphoreType.DMA((8,)),
             pltpu.SemaphoreType.DMA((8,)),
         ],

time: 72.1 us -> 71 us (0.985)
  the two profiles are of different devices: /device:TPU:1 before, /device:TPU:0 now
where the time goes in v4:
time: 71 us; the launch traced here: 70.8 us
  Pallas kernels  70.1 us (99%)
  local copies, waits for them, and re-layouts  0.71 us (1%)
    pallas_call x1, Pallas kernels, back(): pl.pallas_call(back_kernel, out_shape=jax.ShapeDtypeStruct((tokens, FEATU...  35.6 us
    pallas_call x1, Pallas kernels, front(): pl.pallas_call(front_kernel, out_shape=(jax.ShapeDtypeStruct((tokens, lan...  25.8 us
    pallas_call x1, Pallas kernels, attention(): pl.pallas_call(attention_kernel, out_shape=jax.ShapeDtypeStruct((2 * toke...  8.69 us

profile of v4, /device:TPU:0, one launch (start us, length us, event | category | flops | bytes accessed | tf_op | source)
XLA Modules:
  0.0 70.8 jit_solution(3741790416373626792)
XLA Ops:
  0.0 25.8 %front.1 = (bf16[256,512]{1,0:T(8,128)(2,1)}, bf16[256,512]{1,0:T(8,128)(2,1)}, bf16[16,256,256]{2,1,0:T(8,128)(2,1)}) custom-call(bf16[256,4096]{1,0:T(8,128)(2,1)} %x_hbm.1, bf16[256,512]{1,0:T(8,128)(2,1)} %og_hbm.1, bf16[4096,512]{1,0:T(8,128)(2,1)} %wq_hbm.3, bf16[4096,128]{1,0:T(8,128)(2,1)} %wk_hbm.3, bf16[4096,128]{1,0:T(8,128)(2,1)} %wv_hbm.3, ...), custom_call_target="tpu_custom_call" | custom-call | tf_op jit(solution)/shard_map/front/pallas_call | solution.py:293
  25.8 8.7 %attention.1 = bf16[4608,256]{1,0:T(8,128)(2,1)} custom-call(s32[32]{0:T(128)} %span_ref.1, s32[8]{0:T(128)} %length_ref.1, bf16[256,512]{1,0:T(8,128)(2,1)} %get-tuple-element.8.q_hbm, bf16[256,512]{1,0:T(8,128)(2,1)} %get-tuple-element.9.g_hbm, bf16[4096,256]{1,0:T(8,128)(2,1)} %bitcast.3), custom_call_target="tpu_custom_call" | custom-call | tf_op jit(solution)/shard_map/attention/pallas_call | solution.py:767
  34.5 35.6 %back.1 = bf16[256,512]{1,0:T(8,128)(2,1)S(1)} custom-call(bf16[9,2,256,256]{3,2,1,0:T(8,128)(2,1)} %bitcast.2, bf16[4096,512]{1,0:T(8,128)(2,1)} %wq_hbm.3, bf16[4096,128]{1,0:T(8,128)(2,1)} %wk_hbm.3, bf16[4096,128]{1,0:T(8,128)(2,1)} %wv_hbm.3), custom_call_target="tpu_custom_call" | custom-call | tf_op jit(solution)/shard_map/back/pallas_call | solution.py:529
  70.1 0.7 copy.10

commit v5 on v4

--- a/solution.py
+++ b/solution.py
@@ -499,8 +499,8 @@
     for c in range(1, len(PARTS)):
         issue(c)
         rounds[c - 1].relay()
-        if c > 1:
-            cross(c - 2)
+    for c in range(len(PARTS) - 2):
+        cross(c)
     rounds[last].relay()
     cross(last - 1)
     cross(last)
@@ -580,8 +580,6 @@
     ]
     for copy in local:
         copy.start()
-    blank[...] = jnp.zeros_like(blank)
-
     places = []
     for b in range(2):
         c = span_ref[2 * lax.axis_index("ctx") + b]
@@ -592,12 +590,6 @@
             first = jnp.where(c * HALF >= end, end, first)
         places.append((c, first // TILE, c // (TILE // HALF) + 1))
 
-    def reached(p):
-        t = p // (TILE // HALF)
-        return jnp.logical_or(
-            *[jnp.logical_and(t >= low, t < high) for c, low, high in places]
-        )
-
     def rows_at(n):
         return pl.ds(pl.multiple_of(n * HALF, HALF), HALF)
 
@@ -611,35 +603,60 @@
             block, out_hbm.at[rows_at(r + 2 * tokens // HALF), :], stores.at[1]
         )
 
-    @pl.loop(0, spans)
-    def _(r):
-        p = span_ref[r]
-        row_of[p] = r
-
-        @pl.when(reached(p))
+    for r in range(spans):
+        row_of[span_ref[r]] = r
+    (_, first_low, first_high), (_, later_low, later_high) = places
+    each = TILE // HALF
+    last = spans // each
+
+    def fresh(t):
+        return jnp.logical_or(t < first_low, t >= first_high)
+
+    def load(t):
+        for k in range(each):
+            p = t * each + k
+            block_in(row_of[p], p).start()
+
+    @pl.loop(first_low, first_high)
+    def _(t):
+        load(t)
+
+    @pl.loop(later_low, later_high)
+    def _(t):
+        @pl.when(fresh(t))
         def _():
-            block_in(r, p).start()
-
-        @pl.when(jnp.logical_not(reached(p)))
+            load(t)
+
+    blank[...] = jnp.zeros_like(blank)
+
+    @pl.loop(0, last)
+    def _(t):
+        idle = jnp.logical_and(
+            fresh(t), jnp.logical_or(t < later_low, t >= later_high)
+        )
+
+        @pl.when(idle)
         def _():
-            block_out(blank, r).start()
-
-    for c, low, high in places:
-
-        @pl.loop(low, high)
-        def _(t):
-            acc[pl.ds(pl.multiple_of(t * TILE, TILE), TILE), :] = jnp.zeros((TILE, wide), jnp.float32)
+            for k in range(each):
+                block_out(blank, row_of[t * each + k]).start()
+
+    def ready(t):
+        at = pl.ds(pl.multiple_of(t * TILE, TILE), TILE)
+        acc[at, :] = jnp.zeros((TILE, wide), jnp.float32)
+        pltpu.make_async_copy(kv_hbm.at[pl.ds(0, TILE), :], kvs.at[at, :], loads.at[2]).wait()
+
+    @pl.loop(first_low, first_high)
+    def _(t):
+        ready(t)
+
+    @pl.loop(later_low, later_high)
+    def _(t):
+        @pl.when(fresh(t))
+        def _():
+            ready(t)
 
     for copy in local:
         copy.wait()
-
-    @pl.loop(0, spans)
-    def _(r):
-        p = span_ref[r]
-
-        @pl.when(reached(p))
-        def _():
-            block_in(r, p).wait()
 
     lanes = BUNDLE * HALF
     for b in range(2):
@@ -739,18 +756,19 @@
         dkv_ref[to, CHANNEL_DIM:] = acc[at, CHANNEL_DIM:].astype(jnp.bfloat16)
         block_out(dkv_ref.at[to, :], r).start()
 
-    for b, (c, low, high) in enumerate(places):
-
-        @pl.loop(low, high)
-        def _(t):
-            fresh = True
-            if b:
-                fresh = jnp.logical_or(t < places[0][1], t >= places[0][2])
-
-            @pl.when(fresh)
-            def _():
-                for k in range(TILE // HALF):
-                    finish(t * (TILE // HALF) + k)
+    def finish_tile(t):
+        for k in range(each):
+            finish(t * each + k)
+
+    @pl.loop(first_low, first_high)
+    def _(t):
+        finish_tile(t)
+
+    @pl.loop(later_low, later_high)
+    def _(t):
+        @pl.when(fresh(t))
+        def _():
+            finish_tile(t)
 
     grads.wait()
     pltpu.make_async_copy(

time: 71 us -> 70.9 us (level)
  no operation moved by 1% of the time
where the time goes in v5:
time: 70.9 us; the launch traced here: 70.8 us
  Pallas kernels  70.1 us (99%)
  local copies, waits for them, and re-layouts  0.71 us (1%)
    pallas_call x1, Pallas kernels, back(): pl.pallas_call(back_kernel, out_shape=jax.ShapeDtypeStruct((tokens, FEATU...  35.6 us
    pallas_call x1, Pallas kernels, front(): pl.pallas_call(front_kernel, out_shape=(jax.ShapeDtypeStruct((tokens, lan...  25.8 us
    pallas_call x1, Pallas kernels, attention(): pl.pallas_call(attention_kernel, out_shape=jax.ShapeDtypeStruct((2 * toke...  8.66 us

profile of v5, /device:TPU:0, one launch (start us, length us, event | category | flops | bytes accessed | tf_op | source)
XLA Modules:
  0.0 70.8 jit_solution(303591812795223591)
XLA Ops:
  0.0 25.8 %front.1 = (bf16[256,512]{1,0:T(8,128)(2,1)}, bf16[256,512]{1,0:T(8,128)(2,1)}, bf16[16,256,256]{2,1,0:T(8,128)(2,1)}) custom-call(bf16[256,4096]{1,0:T(8,128)(2,1)} %x_hbm.1, bf16[256,512]{1,0:T(8,128)(2,1)} %og_hbm.1, bf16[4096,512]{1,0:T(8,128)(2,1)} %wq_hbm.3, bf16[4096,128]{1,0:T(8,128)(2,1)} %wk_hbm.3, bf16[4096,128]{1,0:T(8,128)(2,1)} %wv_hbm.3, ...), custom_call_target="tpu_custom_call" | custom-call | tf_op jit(solution)/shard_map/front/pallas_call | solution.py:293
  25.8 8.7 %attention.1 = bf16[4608,256]{1,0:T(8,128)(2,1)} custom-call(s32[32]{0:T(128)} %span_ref.1, s32[8]{0:T(128)} %length_ref.1, bf16[256,512]{1,0:T(8,128)(2,1)} %get-tuple-element.8.q_hbm, bf16[256,512]{1,0:T(8,128)(2,1)} %get-tuple-element.9.g_hbm, bf16[4096,256]{1,0:T(8,128)(2,1)} %bitcast.3), custom_call_target="tpu_custom_call" | custom-call | tf_op jit(solution)/shard_map/attention/pallas_call | solution.py:785
  34.5 35.6 %back.1 = bf16[256,512]{1,0:T(8,128)(2,1)S(1)} custom-call(bf16[9,2,256,256]{3,2,1,0:T(8,128)(2,1)} %bitcast.2, bf16[4096,512]{1,0:T(8,128)(2,1)} %wq_hbm.3, bf16[4096,128]{1,0:T(8,128)(2,1)} %wk_hbm.3, bf16[4096,128]{1,0:T(8,128)(2,1)} %wv_hbm.3), custom_call_target="tpu_custom_call" | custom-call | tf_op jit(solution)/shard_map/back/pallas_call | solution.py:529
  70.1 0.7 copy.10
